TPU v7x, 32 devices: a whole 2x2x4 slice. The times are simulated.
32 devices in a mesh: gx: 2 (over y), gy: 4 (over x, core), gz: 4 (over z).
Axes of the slice: x: 2, y: 2, z: 4, core: 2. Of those that a mesh axis runs over, the one named last changes fastest.
Arguments:
- displacement: float32 [3, 4, 16, 512], P(None, 'gx', 'gy', 'gz'), may hold values from -0.4 to 0.4
- load: float32 [3, 4, 16, 512], P(None, 'gx', 'gy', 'gz'), may hold values from -12 to 12
- material: int32 [4, 16, 512], P('gx', 'gy', 'gz'), may hold values from 0 to 7, as said below
- free_node: int32 [4, 16, 512], P('gx', 'gy', 'gz'), may hold values 0 or 1
- table: float32 [8, 3], replicated, may hold values from 0.5 to 20, as said below
Outputs:
- increment: float32 [3, 4, 16, 512], P(None, 'gx', 'gy', 'gz')
- residual: float32 [3, 4, 16, 512], P(None, 'gx', 'gy', 'gz')
Inputs may be any that keep to these rules, and one draw needn't show every extreme that they name: The material id of an element with third index k lies between band and band + 2, where band = (k * 6) // 512. `table`: all entries positive.
All inputs are finite; a program needn't handle non-finite values. No bound on the sum of `free_node` on one device may be relied on, other than what follows from the above.
Results may differ from a plain program's by a relative error of at most 0.0004.
Values sent between devices are 32-bit elements; how exact they have to be, the bound alone decides.
A program may use at most 64 MiB of HBM per device.

v0:
```python
import functools

import jax
import jax.numpy as jnp
from jax import lax
from jax.experimental import pallas as pl
from jax.experimental.pallas import tpu as pltpu
from jax.sharding import PartitionSpec as P

OUTER = 2
SHIFTS = (9.6, 51.4)
HALF_WIDTH = 29.5
CHAIN = SHIFTS + (30.5,) + SHIFTS + (30.5,)
FIELDS = 8
STRIP = 16
ROWS = 16
MESH = pl.DeviceIdType.MESH


def loop(count, body):
    if count <= 8:
        for i in range(count):
            body(i)
    else:

        def step(i, carry):
            body(i)
            return carry

        lax.fori_loop(0, count, step, 0)


def when(condition, body):
    pl.when(condition)(body)


def solve_small(gram, right):
    sym = [[0.5 * (gram[i][j] + gram[j][i]) for j in range(3)] for i in range(3)]
    l00 = jnp.sqrt(sym[0][0])
    l10 = sym[1][0] / l00
    l20 = sym[2][0] / l00
    l11 = jnp.sqrt(sym[1][1] - l10 * l10)
    l21 = (sym[2][1] - l20 * l10) / l11
    l22 = jnp.sqrt(sym[2][2] - l20 * l20 - l21 * l21)
    y0 = right[0] / l00
    y1 = (right[1] - l10 * y0) / l11
    y2 = (right[2] - l20 * y0 - l21 * y1) / l22
    c2 = y2 / l22
    c1 = (y1 - l21 * c2) / l11
    c0 = (y0 - l10 * c1 - l20 * c2) / l00
    return [c0, c1, c2]


def kernel(
    grid,
    shard,
    disp_hbm,
    load_hbm,
    mat_hbm,
    free_hbm,
    table_hbm,
    out_ref,
    blocks,
    from_low,
    from_high,
    to_low,
    to_high,
    basis,
    nodal,
    piola,
    state,
    freeb,
    massb,
    own,
    sums,
    flags,
    table_ref,
    in_sem,
    send_sem,
    recv_sem,
    sum_send,
    sum_recv,
):
    ngx, ngy, ngz = grid
    sx, sy, sz = shard
    nx, ny, nz = ngx * sx, ngy * sy, ngz * sz
    width = sz + 128
    n = ngx * ngy
    gx, gy, gz = lax.axis_index("gx"), lax.axis_index("gy"), lax.axis_index("gz")
    me = gx * ngy + gy
    has_low, has_high = gz > 0, gz < ngz - 1

    def target(p, z):
        return {"gx": p // ngy, "gy": lax.rem(p, ngy), "gz": z}

    def fetch(src, dst, slot):
        return pltpu.make_async_copy(src, dst, in_sem.at[slot])

    fetched = [
        fetch(disp_hbm, blocks.at[me, pl.ds(0, 3)], 0),
        fetch(load_hbm, blocks.at[me, pl.ds(3, 3)], 1),
        fetch(mat_hbm, flags.at[0], 2),
        fetch(free_hbm, flags.at[1], 3),
        fetch(table_hbm, table_ref, 4),
    ]
    for copy in fetched:
        copy.start()

    barrier = pltpu.get_barrier_semaphore()

    def greet(p, z):
        pl.semaphore_signal(barrier, inc=1, device_id=target(p, z), device_id_type=MESH)

    def peers(count, first, body):
        loop(count, lambda k: body(lax.rem(me + first + k, n)))

    peers(n - 1, 1, lambda p: greet(p, gz))
    when(has_low, lambda: peers(n, 0, lambda p: greet(p, gz - 1)))
    when(has_high, lambda: peers(n, 0, lambda p: greet(p, gz + 1)))
    for z in range(ngz):
        when((z > gz + 1) | (z < gz - 1), lambda z=z: greet(me, z))

    for copy in fetched[:4]:
        copy.wait()
    blocks[me, 6] = flags[0].astype(jnp.float32)
    blocks[me, 7] = flags[1].astype(jnp.float32)
    lane = lax.broadcasted_iota(jnp.int32, (sy, 128), 1)
    for i in range(sx):
        low = jnp.zeros((sy, 128), jnp.float32)
        high = jnp.zeros((sy, 128), jnp.float32)
        for f in range(FIELDS):
            part = blocks[me, f, i]
            here = (lane >= STRIP * f) & (lane < STRIP * (f + 1))
            first, last = part[:, :128], part[:, sz - 128 :]
            if f:
                first = pltpu.roll(first, STRIP * f, 1)
            if f < 7:
                last = pltpu.roll(last, STRIP * f + STRIP, 1)
            low = jnp.where(here, first, low)
            high = jnp.where(here, last, high)
        to_low[i] = low
        to_high[i] = high

    def clear(ref):
        ref[...] = jnp.zeros(ref.shape, jnp.float32)

    when(jnp.logical_not(has_low), lambda: clear(from_low))
    when(jnp.logical_not(has_high), lambda: clear(from_high))

    expected = n - 1 + jnp.where(has_low, n, 0) + jnp.where(has_high, n, 0)
    for z in range(ngz):
        expected = expected + jnp.where((z > gz + 1) | (z < gz - 1), 1, 0)
    pl.semaphore_wait(barrier, expected)

    def send(src, dst, slot, p, z):
        pltpu.make_async_remote_copy(
            src_ref=src,
            dst_ref=dst,
            send_sem=send_sem.at[slot],
            recv_sem=recv_sem.at[slot],
            device_id=target(p, z),
            device_id_type=MESH,
        ).start()

    peers(n - 1, 1, lambda p: send(blocks.at[me], blocks.at[me], 0, p, gz))
    when(
        has_high,
        lambda: peers(n, 0, lambda p: send(to_high, from_low.at[me], 1, p, gz + 1)),
    )
    when(
        has_low,
        lambda: peers(n, 0, lambda p: send(to_low, from_high.at[me], 2, p, gz - 1)),
    )

    def settle(ref, sem):
        pltpu.make_async_copy(ref, ref, sem).wait()

    for e in range(9):
        piola[e, 0] = jnp.zeros((ny, width), jnp.float32)
        piola[e, nx] = jnp.zeros((ny, width), jnp.float32)

    settle(blocks.at[pl.ds(0, n - 1)], recv_sem.at[0])
    when(has_low, lambda: settle(from_low, recv_sem.at[1]))
    when(has_high, lambda: settle(from_high, recv_sem.at[2]))

    tail = lax.broadcasted_iota(jnp.int32, (ny, 128), 1)

    def rows(ref, index, x):
        gi, i = x // sx, lax.rem(x, sx) if not isinstance(x, int) else x % sx
        return jnp.concatenate([ref[(gi * ngy + g,) + index + (i,)] for g in range(ngy)], axis=0)

    def whole_rows(f, x, after, before):
        up = after if f == 0 else pltpu.roll(after, 128 - STRIP * f, 1)
        down = before if f == 7 else pltpu.roll(before, 128 - STRIP - STRIP * f, 1)
        halo = jnp.where(tail < STRIP, up, jnp.where(tail >= 128 - STRIP, down, 0.0))
        return jnp.concatenate([rows(blocks, (f,), x), halo], axis=1)

    def unpack(x):
        after, before = rows(from_high, (), x), rows(from_low, (), x)
        free = whole_rows(7, x, after, before)
        freeb[x] = free
        for c in range(3):
            basis[1, c, x] = whole_rows(c, x, after, before)
            basis[0, c, x] = whole_rows(3 + c, x, after, before) * free
        basis[2, 0, x] = whole_rows(6, x, after, before)

    loop(nx, unpack)

    def next_z(v):
        return pltpu.roll(v, width - 1, 1)

    def last_z(v):
        return pltpu.roll(v, 1, 1)

    def next_y(v):
        return pltpu.roll(v, ny - 1, 0)

    def last_y(v):
        return pltpu.roll(v, 1, 0)

    def spread(j, masked):
        def plane(x):
            for c in range(3):
                v = basis[j, c, x]
                if masked:
                    v = v * freeb[x]
                moved = next_z(v)
                total, change = v + moved, moved - v
                shifted = next_y(total)
                nodal[3 * c, x] = total + shifted
                nodal[3 * c + 1, x] = shifted - total
                nodal[3 * c + 2, x] = change + next_y(change)

        loop(nx, plane)

    tiles = [(8 * a, 128 * b) for a in range(ny // 8) for b in range(width // 128)]

    def gradient(e, r, l):
        at = (pl.ds(r, 8), pl.ds(l, 128))
        grad = []
        for c in range(3):
            one = [nodal[(3 * c + d, e) + at] for d in range(3)]
            two = [nodal[(3 * c + d, e + 1) + at] for d in range(3)]
            grad.append([two[0] - one[0], two[1] + one[1], two[2] + one[2]])
        return grad

    pairs = [(0, 0), (0, 1), (0, 2), (1, 1), (1, 2), (2, 2)]

    spread(1, False)
    fetched[4].wait()

    def build(e):
        for r, l in tiles:
            at = (pl.ds(r, 8), pl.ds(l, 128))
            grad = gradient(e, r, l)
            material = basis[(2, 0, e) + at]
            yy = r + lax.broadcasted_iota(jnp.int32, (8, 128), 0)
            zz = l + lax.broadcasted_iota(jnp.int32, (8, 128), 1)
            zz = jnp.where(zz < sz + STRIP, zz, zz - width)
            zg = zz + gz * sz
            valid = (yy <= ny - 2) & (zz >= -STRIP) & (zz <= sz + STRIP - 2)
            valid = valid & (zg >= 0) & (zg <= nz - 2)
            zero = jnp.zeros((8, 128), jnp.float32)
            lame, shear, mass = zero, zero, zero
            for row in range(table_ref.shape[1]):
                hit = material == float(row)
                lame = jnp.where(hit, table_ref[0, row], lame)
                shear = jnp.where(hit, table_ref[1, row], shear)
                mass = jnp.where(hit, table_ref[2, row], mass)
            lame = jnp.where(valid, lame * 0.0625, 0.0)
            shear = jnp.where(valid, shear * 0.0625, 0.0)
            basis[(3, 0, e) + at] = jnp.where(valid, mass * 0.125, 0.0)
            frame = [
                [0.25 * grad[i][j] + (1.0 if i == j else 0.0) for j in range(3)] for i in range(3)
            ]
            strain = {}
            for i, j in pairs:
                v = sum(frame[k][i] * frame[k][j] for k in range(3))
                strain[i, j] = 0.5 * (v - 1.0 if i == j else v)
            bulk = lame * (strain[0, 0] + strain[1, 1] + strain[2, 2])
            for i in range(3):
                for j in range(3):
                    state[(3 * i + j, e) + at] = frame[i][j]
            for place, (i, j) in enumerate(pairs):
                v = 2.0 * shear * strain[i, j]
                state[(9 + place, e) + at] = v + bulk if i == j else v
            state[(15, e) + at] = lame
            state[(16, e) + at] = shear

    loop(nx - 1, build)

    basis[3, 0, nx - 1] = jnp.zeros((ny, width), jnp.float32)
    massb[0] = basis[3, 0, 0]
    loop(nx - 1, lambda x: massb.__setitem__(x + 1, basis[3, 0, x + 1] + basis[3, 0, x]))

    def lump(x):
        v = massb[x]
        v = v + last_y(v)
        massb[x] = v + last_z(v)

    loop(nx, lump)

    def apply(j):
        spread(j, True)

        def stress(e):
            for r, l in tiles:
                at = (pl.ds(r, 8), pl.ds(l, 128))
                g = gradient(e, r, l)
                f = [[state[(3 * i + k, e) + at] for k in range(3)] for i in range(3)]
                pulled = [
                    [sum(f[k][a] * g[k][b] for k in range(3)) for b in range(3)] for a in range(3)
                ]
                lame, shear = state[(15, e) + at], state[(16, e) + at]
                bulk = lame * (pulled[0][0] + pulled[1][1] + pulled[2][2])
                t, s = {}, {}
                for place, (a, b) in enumerate(pairs):
                    v = shear * (pulled[a][b] + pulled[b][a])
                    t[a, b] = t[b, a] = v + bulk if a == b else v
                    s[a, b] = s[b, a] = state[(9 + place, e) + at]
                for i in range(3):
                    for b in range(3):
                        v = sum(f[i][k] * t[k, b] for k in range(3))
                        w = sum(g[i][k] * s[k, b] for k in range(3))
                        piola[(3 * i + b, e + 1) + at] = v + w

        loop(nx - 1, stress)

        def gather(x):
            free = freeb[x]
            fixed = 1.0 - free
            for c in range(3):
                across = piola[3 * c, x] - piola[3 * c, x + 1]
                along = piola[3 * c + 1, x] + piola[3 * c + 1, x + 1]
                up = piola[3 * c + 2, x] + piola[3 * c + 2, x + 1]
                flat = last_y(across + along) + (across - along)
                up = up + last_y(up)
                v = basis[j, c, x]
                out = last_z(flat + up) + (flat - up) + massb[x] * v
                out = free * out + fixed * v
                basis[j + 1, c, x] = (out - CHAIN[j] * v) * (1.0 / HALF_WIDTH)

        loop(nx, gather)

    def times(coords):
        out = [None] * 7
        for k in range(7):
            if coords[k] is not None:
                out[k] = add(out[k], CHAIN[k] * coords[k])
                out[k + 1] = add(out[k + 1], HALF_WIDTH * coords[k])
        return out

    def add(p, q):
        return q if p is None else p if q is None else p + q

    def scaled(factor, coords):
        return [None if q is None else factor * q for q in coords]

    def plus(p, q):
        return [add(u, w) for u, w in zip(p, q)]

    def combine(coords, vectors):
        return sum(q * w for q, w in zip(coords, vectors) if q is not None)

    def krylov(start):
        b, m = [start], []
        for j in range(3):
            m.append(times(b[j]))
            if j < 2:
                b.append(
                    scaled(1.0 / HALF_WIDTH, plus(m[j], scaled(-SHIFTS[j], b[j])))
                )
        return b, m

    def inner(o, start, images):
        entries = [(i, j) for i in range(3) for j in range(3)]
        if o:
            wide = [
                [None if q is None else jnp.broadcast_to(q, (8, 128)) for q in coords]
                for coords in [start] + images
            ]

        def plane(x, acc):
            acc = list(acc)
            for c in range(3):
                for r in range(ny // 8):
                    for l in range(sz // 128):
                        at = (pl.ds(8 * r, 8), pl.ds(128 * l, 128))
                        v = [basis[(k, c, x) + at] for k in range(7 if o else 4)]
                        if o:
                            b = [combine(wide[0], v)]
                            m = [combine(wide[1 + j], v) for j in range(3)]
                            for j in range(2):
                                b.append((m[j] - SHIFTS[j] * b[j]) * (1.0 / HALF_WIDTH))
                        else:
                            b = v[:3]
                            m = [HALF_WIDTH * v[j + 1] + CHAIN[j] * v[j] for j in range(3)]
                        for k, (i, j) in enumerate(entries):
                            acc[k] = acc[k] + b[i] * m[j]
                        for i in range(3):
                            acc[9 + i] = acc[9 + i] + b[i] * b[0]
            return tuple(acc)

        acc = tuple(jnp.zeros((8, 128), jnp.float32) for k in range(12))
        if nx <= 8:
            for x in range(nx):
                acc = plane(x, acc)
        else:
            acc = lax.fori_loop(0, nx, plane, acc)
        for k in range(12):
            sums[o, gz, k : k + 1, :] = jnp.sum(acc[k], axis=0, keepdims=True)
        sums[o, gz, 12:ROWS, :] = jnp.zeros((ROWS - 12, 128), jnp.float32)
        for k in range(1, ngz):
            pltpu.make_async_remote_copy(
                src_ref=sums.at[o, gz],
                dst_ref=sums.at[o, gz],
                send_sem=sum_send.at[o],
                recv_sem=sum_recv.at[o],
                device_id={"gx": gx, "gy": gy, "gz": lax.rem(gz + k, ngz)},
                device_id_type=MESH,
            ).start()

    def coefficients(o):
        settle(sums.at[o, pl.ds(0, ngz - 1)], sum_recv.at[o])
        total = sums[o, 0]
        for z in range(1, ngz):
            total = total + sums[o, z]
        total = jnp.sum(total, axis=1, keepdims=True)
        value = [total[k : k + 1, :] for k in range(12)]
        return solve_small([value[0:3], value[3:6], value[6:9]], value[9:12])

    for j in range(3):
        apply(j)
    inner(0, None, None)
    for j in range(3, 6):
        apply(j)
    coeffs = coefficients(0)
    one = jnp.ones((1, 1), jnp.float32)
    b, m = krylov([one] + [None] * 6)
    start, gain = b[0], [None] * 7
    for j in range(3):
        gain = plus(gain, scaled(coeffs[j], b[j]))
        start = plus(start, scaled(-coeffs[j], m[j]))
    b, m = krylov(start)
    inner(1, start, m)
    coeffs = coefficients(1)
    left = start
    for j in range(3):
        gain = plus(gain, scaled(coeffs[j], b[j]))
        left = plus(left, scaled(-coeffs[j], m[j]))
    for slot, coords in ((0, gain), (1, left)):
        for c in range(3):
            for i in range(sx):
                x = gx * sx + i
                v = combine(coords, [basis[k, c, x, :, pl.ds(0, sz)] for k in range(7)])
                for g in range(ngy):
                    own[slot, c, i, g] = v[g * sy : (g + 1) * sy]
                out_ref[slot, c, i] = own[slot, c, i, gy]

    settle(blocks.at[pl.ds(0, n - 1)], send_sem.at[0])
    when(has_high, lambda: settle(from_low, send_sem.at[1]))
    when(has_low, lambda: settle(from_high, send_sem.at[2]))
    for o in range(OUTER):
        settle(sums.at[o, pl.ds(0, ngz - 1)], sum_send.at[o])


def per_device(displacement, load, material, free_node, table):
    shard = displacement.shape[1:]
    sx, sy, sz = shard
    grid = tuple(lax.axis_size(a) for a in ("gx", "gy", "gz"))
    n = grid[0] * grid[1]
    nx, ny, width = grid[0] * sx, grid[1] * sy, sz + 128
    f32 = jnp.float32
    out = jax.ShapeDtypeStruct((2,) + displacement.shape, f32)
    vmem = pl.BlockSpec(memory_space=pltpu.VMEM)
    buffers = [
        (n, FIELDS, sx, sy, sz),
        (n, sx, sy, 128),
        (n, sx, sy, 128),
        (sx, sy, 128),
        (sx, sy, 128),
        (7, 3, nx, ny, width),
        (9, nx, ny, width),
        (9, nx + 1, ny, width),
        (17, nx - 1, ny, width),
        (nx, ny, width),
        (nx, ny, width),
        (2, 3, sx, grid[1], sy, sz),
        (OUTER, grid[2], ROWS, 128),
    ]
    both = pl.pallas_call(
        functools.partial(kernel, grid, shard),
        out_shape=out,
        in_specs=[pl.BlockSpec(memory_space=pltpu.HBM)] * 5,
        out_specs=vmem,
        scratch_shapes=[
            *(pltpu.VMEM(b, f32) for b in buffers),
            pltpu.VMEM((2, sx, sy, sz), jnp.int32),
            pltpu.SMEM(table.shape[::-1], f32),
            pltpu.SemaphoreType.DMA((5,)),
            pltpu.SemaphoreType.DMA((3,)),
            pltpu.SemaphoreType.DMA((3,)),
            pltpu.SemaphoreType.DMA((OUTER,)),
            pltpu.SemaphoreType.DMA((OUTER,)),
        ],
        compiler_params=pltpu.CompilerParams(
            collective_id=0, has_side_effects=True, vmem_limit_bytes=67043328
        ),
    )(displacement, load, material, free_node, table.T)
    return both[0], both[1]


def solution(mesh):
    in_specs = (
        P(None, "gx", "gy", "gz"),
        P(None, "gx", "gy", "gz"),
        P("gx", "gy", "gz"),
        P("gx", "gy", "gz"),
        P(),
    )
    out_specs = (P(None, "gx", "gy", "gz"), P(None, "gx", "gy", "gz"))
    return jax.shard_map(
        per_device, mesh=mesh, in_specs=in_specs, out_specs=out_specs, check_vma=False
    )
```

profile of v0, /device:TPU:0, one launch (start us, length us, event | category | flops | bytes accessed | tf_op | source)
XLA Modules:
  0.0 23.2 jit_solution(15447814460515153752)
XLA Ops:
  0.6 21.2 %shard_map.68 = f32[2,3,2,4,128]{4,3,2,1,0:T(4,128)} custom-call(f32[3,2,4,128]{3,2,1,0:T(4,128)} %disp_hbm.1, f32[3,2,4,128]{3,2,1,0:T(4,128)} %load_hbm.1, s32[2,4,128]{2,1,0:T(4,128)} %mat_hbm.1, s32[2,4,128]{2,1,0:T(4,128)} %free_hbm.1, f32[3,8]{1,0:T(4,128)} %bitcast.5), custom_call_target="tpu_custom_call" | custom-call | tf_op jit(solution)/shard_map/pallas_call | solution.py:491
  21.8 1.3 %slice_bitcast_fusion = (f32[3,2,4,128]{3,2,1,0:T(4,128)}, f32[3,2,4,128]{3,2,1,0:T(4,128)}) fusion(f32[2,3,2,4,128]{4,3,2,1,0:T(4,128)} %shard_map.68), kind=kLoop, calls=%fused_computation | loop fusion | bytes 49152 | tf_op jit(solution)/shard_map/squeeze | solution.py:510
where the time goes:
time: 23.5 us; the launch traced here: 23.2 us
  Pallas kernels  21.2 us (90%)
  local copies, waits for them, and re-layouts  1.33 us (6%)
  between operations  0.64 us (3%)
    pallas_call x1, Pallas kernels, per_device(): pl.pallas_call(functools.partial(kernel, grid, shard), out_shape=out, in_...  21.2 us
    squeeze x1, local copies, waits for them, and re-layouts, per_device(): return (both[0], both[1])  1.33 us

commit v1 on v0

v1 whole, which is shorter than its diff:
```python
import functools

import jax
import jax.numpy as jnp
import numpy as np
from jax import lax
from jax.experimental import pallas as pl
from jax.experimental.pallas import tpu as pltpu
from jax.sharding import PartitionSpec as P

SHIFTS = (9.6, 51.4)
HALF_WIDTH = 29.5
CHAIN = SHIFTS + (30.5,) + SHIFTS + (30.5,)
STEPS = 6
FIELDS = 8
LANES = 128
PRODUCTS = [(i, j) for i in range(7) for j in range(i, 7) if i < 6]
F32 = jnp.float32


def place(t):
    return 32 * (t // 8) + t % 8


def tables():
    def times(x):
        out = np.zeros(7)
        for k in range(6):
            out[k] += CHAIN[k] * x[k]
            out[k + 1] += HALF_WIDTH * x[k]
        return out

    unit = np.eye(7)
    start = [unit[0]] + [-times(unit[j]) for j in range(3)]
    b, m = [start], []
    for j in range(3):
        m.append([times(x) for x in b[j]])
        if j < 2:
            b.append([(y - SHIFTS[j] * x) / HALF_WIDTH for x, y in zip(b[j], m[j])])
    forms = [(b[i], m[j]) for i in range(3) for j in range(3)] + [(b[i], start) for i in range(3)]
    wide = np.zeros((4, 4, 16, LANES))
    for f, (left, right) in enumerate(forms):
        for a in range(4):
            for t, (i, j) in enumerate(PRODUCTS):
                wide[0, a, f, place(t)] = left[a][i]
                wide[1, a, f, place(t)] = left[a][j] if i != j else 0.0
                wide[2, a, f, place(t)] = right[a][i]
                wide[3, a, f, place(t)] = right[a][j]
    last = np.zeros((16, LANES))
    for a in range(4):
        for k in range(7):
            last[a, k] = 1.0 if 0 < a == k + 1 else 0.0
            last[a, 16 + k] = start[a][k]
            for j in range(3):
                last[4 + 4 * j + a, k] = b[j][a][k]
                last[4 + 4 * j + a, 16 + k] = -m[j][a][k]
    return np.concatenate([wide.reshape(-1, LANES), last]).astype(np.float32)


def solve_small(gram, right):
    sym = [[0.5 * (gram[i][j] + gram[j][i]) for j in range(3)] for i in range(3)]
    l00 = jnp.sqrt(sym[0][0])
    l10 = sym[1][0] / l00
    l20 = sym[2][0] / l00
    l11 = jnp.sqrt(sym[1][1] - l10 * l10)
    l21 = (sym[2][1] - l20 * l10) / l11
    l22 = jnp.sqrt(sym[2][2] - l20 * l20 - l21 * l21)
    y0 = right[0] / l00
    y1 = (right[1] - l10 * y0) / l11
    y2 = (right[2] - l20 * y0 - l21 * y1) / l22
    c2 = y2 / l22
    c1 = (y1 - l21 * c2) / l11
    c0 = (y0 - l10 * c1 - l20 * c2) / l00
    return [c0, c1, c2]


def two_sum(a, b):
    s = a + b
    t = s - a
    return s, (a - (s - t)) + (b - t)


def add_pair(p, q):
    s, e = two_sum(p[0], q[0])
    return s, e + (p[1] + q[1])


def split(a):
    t = 4097.0 * a
    high = t - (t - a)
    return high, a - high


def two_product(a, b):
    p = a * b
    (ah, al), (bh, bl) = split(a), split(b)
    return p, ((ah * bh - p) + ah * bl + al * bh) + al * bl


def loop(count, body):
    if count <= 32:
        for i in range(count):
            body(i)
    else:

        def step(i, carry):
            body(i)
            return carry

        lax.fori_loop(0, count, step, 0)


def when(condition, body):
    if isinstance(condition, bool):
        if condition:
            body()
    else:
        pl.when(condition)(body)


class Plan:
    def __init__(self, grid, shard):
        self.grid, self.shard = grid, shard
        ngx, ngy, ngz = grid
        sx, sy, sz = shard
        self.n = ngx * ngy
        self.nz = ngz * sz
        self.halo = STEPS
        self.counts = [self.n] * ngz
        self.own = -(-self.nz // sum(self.counts))
        self.span = self.own + 2 * self.halo
        self.pitch = 1 << (self.span - 1).bit_length()
        self.packed = LANES // self.pitch
        self.groups = ngx * sx // self.packed
        self.mixed = LANES // (sx * self.pitch)
        self.tiles = FIELDS // self.mixed
        self.stride = LANES // (3 * sx)
        self.workers = -(-self.nz // self.own)
        self.base = [sum(self.counts[:z]) for z in range(ngz)]
        own, halo = self.own, self.halo
        self.to_low = [max(0, (sz * z - own - halo) // own + 1) for z in range(ngz)]
        self.to_high = [
            min(self.workers - 1, -(-(sz * z + sz + halo) // own) - 1) for z in range(ngz)
        ]
        self.from_low = [sz * z // own for z in range(ngz)]
        self.from_high = [(sz * z + sz - 1) // own for z in range(ngz)]
        self.sends = max(b - a + 1 for a, b in zip(self.to_low, self.to_high))
        self.returns = max(b - a + 1 for a, b in zip(self.from_low, self.from_high))
        assert sz == LANES and 8 % sy == 0 and own <= self.stride and LANES % self.pitch == 0


def pick(values, z):
    if all(v == values[0] for v in values):
        return values[0]
    out = values[0]
    for k in range(1, len(values)):
        out = jnp.where(z >= k, values[k], out)
    return out


def kernel(
    plan,
    disp_hbm,
    load_hbm,
    mat_hbm,
    free_hbm,
    table_hbm,
    const_hbm,
    out_ref,
    raw,
    flags,
    pack,
    recv,
    basis,
    fields,
    state,
    parts,
    back,
    vt,
    sums,
    const,
    table_ref,
    in_sem,
    send_sem,
    recv_sem,
    back_send,
    back_recv,
    sum_send,
    sum_recv,
):
    ngx, ngy, ngz = plan.grid
    sx, sy, sz = plan.shard
    n, own, halo, pitch = plan.n, plan.own, plan.halo, plan.pitch
    nx, ny = ngx * sx, ngy * sy
    groups, mixed, tiles = plan.groups, plan.mixed, plan.tiles
    total = n * ngz
    gx, gy, gz = lax.axis_index("gx"), lax.axis_index("gy"), lax.axis_index("gz")
    p = gx * ngy + gy
    me = p * ngz + gz
    worker = pick(plan.base, gz) + p
    first = own * worker - halo

    fetched = [
        pltpu.make_async_copy(disp_hbm, raw.at[pl.ds(0, 3)], in_sem.at[0]),
        pltpu.make_async_copy(load_hbm, raw.at[pl.ds(3, 3)], in_sem.at[1]),
        pltpu.make_async_copy(mat_hbm, flags.at[0], in_sem.at[2]),
        pltpu.make_async_copy(free_hbm, flags.at[1], in_sem.at[3]),
        pltpu.make_async_copy(table_hbm, table_ref, in_sem.at[4]),
        pltpu.make_async_copy(const_hbm, const, in_sem.at[5]),
    ]
    for copy in fetched:
        copy.start()

    def other(k):
        d = me + k
        return jnp.where(d >= total, d - total, d)

    def address(d):
        return {"gx": d // (ngy * ngz), "gy": lax.rem(d // ngz, ngy), "gz": lax.rem(d, ngz)}

    def where_is(d):
        return dict(device_id=d, device_id_type=pl.DeviceIdType.LOGICAL)

    barrier = pltpu.get_barrier_semaphore()
    loop(total - 1, lambda k: pl.semaphore_signal(barrier, inc=1, **where_is(other(k + 1))))

    for copy in fetched[:4]:
        copy.wait()
    raw[6] = flags[0].astype(F32)
    raw[7] = flags[1].astype(F32)

    lane = lax.broadcasted_iota(jnp.int32, (8, LANES), 1)
    row = lax.broadcasted_iota(jnp.int32, (8, LANES), 0)
    per = 8 // sy
    stacks = -(-tiles // per)
    held = []
    for t in range(stacks):
        part = []
        for e in range(mixed * sx):
            f, i = e // sx, e % sx
            rows = [raw[mixed * min(per * t + h, tiles - 1) + f, i] for h in range(per)]
            part.append(jnp.concatenate(rows, axis=0))
        held.append(part)

    to_low = pick(plan.to_low, gz)
    to_count = pick([b - a + 1 for a, b in zip(plan.to_low, plan.to_high)], gz)

    def home(w):
        z = 0
        for k in range(1, ngz):
            z = z + jnp.where(w >= plan.base[k], 1, 0)
        return (w - pick(plan.base, z)) * ngz + z

    def prepare(j):
        w = to_low + j
        offset = sz * gz - (own * w - halo)
        for t in range(stacks):
            out = None
            for e, v in enumerate(held[t]):
                moved = pltpu.roll(v, lax.rem(offset + (pitch * e + 8 * LANES), LANES), 1)
                out = moved if out is None else jnp.where(lane >= pitch * e, moved, out)
            for h in range(min(per, tiles - per * t)):
                pack[j, per * t + h] = out[sy * h : sy * (h + 1)]

    loop(plan.sends, prepare)

    pl.semaphore_wait(barrier, total - 1)

    def piece(j, start):
        w = to_low + j
        slot = jnp.where(sz * gz > jnp.maximum(own * w - halo, 0), 1, 0)
        d = home(w)
        dst = recv.at[slot, :, gx, gy]
        remote = pltpu.make_async_remote_copy(
            src_ref=pack.at[j],
            dst_ref=dst,
            send_sem=send_sem.at[0],
            recv_sem=recv_sem.at[slot],
            **where_is(d),
        )
        valid = True if plan.sends == min(
            b - a + 1 for a, b in zip(plan.to_low, plan.to_high)
        ) else j < to_count
        if start:
            when(valid & (d != me), remote.start)
            when(
                valid & (d == me),
                lambda: pltpu.make_async_copy(pack.at[j], dst, recv_sem.at[slot]).start(),
            )
        else:
            when(valid & (d != me), remote.wait_send)

    loop(plan.sends, lambda j: piece(j, True))

    def settle(ref, sem):
        pltpu.make_async_copy(ref, ref, sem).wait()

    settled = jnp.maximum(first, 0)
    low_slab = lax.div(settled, sz)
    edge = sz * (low_slab + 1)
    two = (first + plan.span > edge) & (low_slab + 1 < ngz)
    settle(recv.at[0], recv_sem.at[0])
    when(two, lambda: settle(recv.at[1], recv_sem.at[1]))

    wide_lane = lax.broadcasted_iota(jnp.int32, (ny, LANES), 1)
    depth = lax.rem(wide_lane, pitch)
    plane = depth + first
    near = plane < edge
    seg = sx * pitch

    def gather_rows(slot, k, x):
        return jnp.concatenate([recv[slot, k, x, g] for g in range(ngy)], axis=0)

    def source(k, x):
        return jnp.where(near, gather_rows(0, k, x), gather_rows(1, k, x))

    def unpack(k, g):
        parts_in = [source(k, g * mixed + d) for d in range(mixed)]
        out = []
        for f in range(mixed):
            v = None
            for d in range(mixed):
                s = (d - f) * seg % LANES
                moved = pltpu.roll(parts_in[d], s, 1) if s else parts_in[d]
                v = moved if v is None else jnp.where(wide_lane >= d * seg, moved, v)
            out.append(v)
        return out

    got = [[None] * groups for _ in range(FIELDS)]
    for g in range(groups):
        for k in range(tiles):
            for f, v in enumerate(unpack(k, g)):
                got[mixed * k + f][g] = v

    span = range(groups)

    def next_z(a):
        return [pltpu.roll(v, LANES - 1, 1) for v in a]

    def last_z(a):
        return [pltpu.roll(v, 1, 1) for v in a]

    def next_y(a):
        return [pltpu.roll(v, ny - 1, 0) for v in a]

    def last_y(a):
        return [pltpu.roll(v, 1, 0) for v in a]

    def next_x(a):
        moved = [pltpu.roll(v, LANES - pitch, 1) for v in a]
        if groups == 1:
            return moved
        return [
            jnp.where(wide_lane >= LANES - pitch, moved[min(g + 1, groups - 1)], moved[g])
            for g in span
        ]

    def last_x(a):
        moved = [pltpu.roll(v, pitch, 1) for v in a]
        if groups == 1:
            return moved
        return [jnp.where(wide_lane < pitch, moved[max(g - 1, 0)], moved[g]) for g in span]

    def both(op, *lists):
        return [op(*vs) for vs in zip(*lists)]

    add = functools.partial(both, lambda a, b: a + b)
    sub = functools.partial(both, lambda a, b: a - b)

    def gradient(vector):
        grad = []
        for v in vector:
            moved = next_z(v)
            total_z, change = add(v, moved), sub(moved, v)
            shifted = next_y(total_z)
            flat, tilt, rise = add(total_z, shifted), sub(shifted, total_z), add(change, next_y(change))
            grad.append(
                [sub(next_x(flat), flat), add(next_x(tilt), tilt), add(next_x(rise), rise)]
            )
        return grad

    pairs = [(0, 0), (0, 1), (0, 2), (1, 1), (1, 2), (2, 2)]
    free = got[7]
    for c in range(3):
        for g in span:
            basis[0, c, g] = got[3 + c][g] * free[g]
    grad = gradient([got[0], got[1], got[2]])
    fetched[4].wait()
    mass = []
    high = lax.broadcasted_iota(jnp.int32, (ny, LANES), 0)
    for g in span:
        valid = (high <= ny - 2) & (plane >= 0) & (plane <= plan.nz - 2) & (depth <= plan.span - 2)
        valid = valid & (lax.div(wide_lane, pitch) + g * plan.packed <= nx - 2)
        material = got[6][g]
        zero = jnp.zeros((ny, LANES), F32)
        lame, shear, heavy = zero, zero, zero
        for r in range(table_ref.shape[1]):
            hit = material == float(r)
            lame = jnp.where(hit, table_ref[0, r], lame)
            shear = jnp.where(hit, table_ref[1, r], shear)
            heavy = jnp.where(hit, table_ref[2, r], heavy)
        lame = jnp.where(valid, lame * 0.0625, 0.0)
        shear = jnp.where(valid, shear * 0.0625, 0.0)
        mass.append(jnp.where(valid, heavy * 0.125, 0.0))
        frame = [
            [0.25 * grad[i][j][g] + (1.0 if i == j else 0.0) for j in range(3)] for i in range(3)
        ]
        strain = {}
        for i, j in pairs:
            v = sum(frame[k][i] * frame[k][j] for k in range(3))
            strain[i, j] = 0.5 * (v - 1.0 if i == j else v)
        bulk = lame * (strain[0, 0] + strain[1, 1] + strain[2, 2])
        for i in range(3):
            for j in range(3):
                state[3 * i + j, g] = frame[i][j]
        for spot, (i, j) in enumerate(pairs):
            v = 2.0 * shear * strain[i, j]
            state[9 + spot, g] = v + bulk if i == j else v
        state[15, g] = lame
        state[16, g] = shear
    mass = add(mass, last_x(mass))
    mass = add(mass, last_y(mass))
    mass = add(mass, last_z(mass))
    for g in span:
        fields[0, g] = free[g]
        fields[1, g] = free[g] * (1.0 / HALF_WIDTH)
        fields[2, g] = (free[g] * mass[g] + (1.0 - free[g])) * (1.0 / HALF_WIDTH)

    rows8 = [pl.ds(8 * r, 8) for r in range(ny // 8)]

    def apply(j):
        grad = gradient([[basis[j, c, g] * fields[0, g] for g in span] for c in range(3)])
        pio = [[[[None] * len(rows8) for _ in span] for _ in range(3)] for _ in range(3)]
        for g in span:
            for r, at in enumerate(rows8):
                d = [[grad[c][q][g][8 * r : 8 * r + 8] for q in range(3)] for c in range(3)]
                f = [[state[3 * i + k, g, at] for k in range(3)] for i in range(3)]
                pulled = [
                    [sum(f[k][a] * d[k][b] for k in range(3)) for b in range(3)] for a in range(3)
                ]
                lame, shear = state[15, g, at], state[16, g, at]
                bulk = lame * (pulled[0][0] + pulled[1][1] + pulled[2][2])
                t, s = {}, {}
                for spot, (a, b) in enumerate(pairs):
                    v = shear * (pulled[a][b] + pulled[b][a])
                    t[a, b] = t[b, a] = v + bulk if a == b else v
                    s[a, b] = s[b, a] = state[9 + spot, g, at]
                for i in range(3):
                    for b in range(3):
                        v = sum(f[i][k] * t[k, b] for k in range(3))
                        pio[i][b][g][r] = v + sum(d[i][k] * s[k, b] for k in range(3))
        for c in range(3):
            e = [[jnp.concatenate(pio[c][b][g], axis=0) for g in span] for b in range(3)]
            across = sub(last_x(e[0]), e[0])
            along = add(last_x(e[1]), e[1])
            up = add(last_x(e[2]), e[2])
            flat = add(last_y(add(across, along)), sub(across, along))
            up = add(up, last_y(up))
            out = add(last_z(add(flat, up)), sub(flat, up))
            for g in span:
                basis[j + 1, c, g] = fields[1, g] * out[g] + (
                    fields[2, g] - CHAIN[j] / HALF_WIDTH
                ) * basis[j, c, g]

    for j in range(STEPS):
        apply(j)

    mine = (depth >= halo) & (depth < halo + own) & (plane < plan.nz)
    spots = [(c, g, r) for c in range(3) for g in span for r in range(ny // 8)]
    for k in range(7):
        v = [
            jnp.where(mine[8 * r : 8 * r + 8], basis[k, c, g, rows8[r]], 0.0) for c, g, r in spots
        ]
        top = jnp.abs(v[0])
        for u in v[1:]:
            top = jnp.maximum(top, jnp.abs(u))
        grain = top * (32768.0 * max(1, len(v) // 6))
        for s, u in enumerate(v):
            coarse = (u + grain) - grain
            parts[0, k, s] = coarse
            parts[1, k, s] = u - coarse
    pairs_of = {}
    for i in range(6):
        acc = {j: [None, None] for j in range(i, 7)}
        for s in range(len(spots)):
            ch, cl = parts[0, i, s], parts[1, i, s]
            for j in range(i, 7):
                dh, dl = parts[0, j, s], parts[1, j, s]
                new = [ch * dh, cl * (dh + ch + dl) if i == j else ch * dl + cl * (dh + dl)]
                acc[j] = new if s == 0 else [acc[j][0] + new[0], acc[j][1] + new[1]]
        for j in range(i, 7):
            pairs_of[i, j] = acc[j]
    items = [tuple(pairs_of[q]) for q in PRODUCTS]
    blank = (jnp.zeros((8, LANES), F32), jnp.zeros((8, LANES), F32))
    items = items + [blank] * (32 - len(items))

    def merge(a, b, mask, shift, axis):
        size = 8 if axis == 0 else LANES
        first_in, second_in = [], []
        for u, v in zip(a, b):
            if 2 * shift == size:
                first_in.append(jnp.where(mask, u, v))
                second_in.append(pltpu.roll(jnp.where(mask, v, u), shift, axis))
            else:
                first_in.append(jnp.where(mask, u, pltpu.roll(v, shift, axis)))
                second_in.append(jnp.where(mask, pltpu.roll(u, size - shift, axis), v))
        return add_pair(first_in, second_in)

    tall = []
    for q in range(4):
        it = items[8 * q : 8 * q + 8]
        one = [merge(it[r], it[r + 4], row < 4, 4, 0) for r in range(4)]
        twice = [merge(one[r], one[r + 2], lax.rem(row, 4) < 2, 2, 0) for r in range(2)]
        tall.append(merge(twice[0], twice[1], lax.rem(row, 2) < 1, 1, 0))
    half = [merge(tall[q], tall[q + 2], lane < 64, 64, 1) for q in range(2)]
    whole = merge(half[0], half[1], lax.rem(lane, 64) < 32, 32, 1)
    for s in (16, 8, 4, 2, 1):
        whole = add_pair(whole, [pltpu.roll(u, LANES - s, 1) for u in whole])
    spread = [pltpu.roll(u, 0, 1, stride=1, stride_axis=0) for u in whole]
    keep = lax.rem(lane, 32) == row
    flat = jnp.where(keep, spread[0], 0.0) + pltpu.roll(jnp.where(keep, spread[1], 0.0), 8, 1)
    sums[me] = jnp.sum(flat, axis=0, keepdims=True)

    def share(k, start):
        copy = pltpu.make_async_remote_copy(
            src_ref=sums.at[me],
            dst_ref=sums.at[me],
            send_sem=sum_send.at[0],
            recv_sem=sum_recv.at[0],
            **where_is(other(k)),
        )
        copy.start()

    loop(total - 1, lambda k: share(k + 1, True))

    stride = plan.stride
    for k in range(1, 7):
        for x in range(ngx):
            g, d = x // mixed, x % mixed
            out = None
            for c in range(3):
                for i in range(sx):
                    e = c * sx + i
                    s = (e * stride - ((d * sx + i) * pitch + halo)) % LANES
                    v = basis[k, c, g]
                    moved = pltpu.roll(v, s, 1) if s else v
                    out = moved if out is None else jnp.where(wide_lane >= e * stride, moved, out)
            for y in range(ngy):
                back[x, y, k - 1] = out[sy * y : sy * (y + 1)]

    own_low = lax.div(own * worker, sz)
    own_high = lax.div(jnp.minimum(own * worker + own, plan.nz) - 1, sz)
    straddles = sz % own != 0

    def give(q, start):
        x, y = (q // ngy, q % ngy) if isinstance(q, int) else (lax.div(q, ngy), lax.rem(q, ngy))

        def to(z):
            d = q * ngz + z
            dst = vt.at[worker - pick(plan.from_low, z)]
            remote = pltpu.make_async_remote_copy(
                src_ref=back.at[x, y],
                dst_ref=dst,
                send_sem=back_send.at[0],
                recv_sem=back_recv.at[0],
                **where_is(d),
            )
            if start:
                when(d != me, remote.start)
                when(
                    d == me,
                    lambda: pltpu.make_async_copy(back.at[x, y], dst, back_recv.at[0]).start(),
                )
            else:
                when(d != me, remote.wait_send)

        to(own_low)
        if straddles:
            when(own_high > own_low, lambda: to(own_high))

    loop(n, lambda q: give(q, True))
    fetched[5].wait()

    counts = [b - a + 1 for a, b in zip(plan.from_low, plan.from_high)]
    if min(counts) == plan.returns:
        settle(vt, back_recv.at[0])
    else:
        for z in range(ngz):
            when(gz == z, lambda z=z: settle(vt.at[pl.ds(0, counts[z])], back_recv.at[0]))

    mates = [(k, c, i) for k in range(0, 6, 2) for c in range(3) for i in range(sx)]

    def collect(j, accs):
        w = pick(plan.from_low, gz) + j
        offset = own * w - sz * gz
        inside = (lane >= offset) & (lane < offset + own)
        if min(counts) != plan.returns:
            inside = inside & (j < pick(counts, gz))
        new = []
        stacked = [jnp.concatenate([vt[j, k], vt[j, k + 1]], axis=0) for k in range(0, 6, 2)]
        for (k, c, i), acc in zip(mates, accs):
            s = lax.rem(offset - (c * sx + i) * stride + 2 * LANES, LANES)
            moved = pltpu.roll(stacked[k // 2], s, 1)
            new.append(jnp.where(inside, moved, acc))
        return tuple(new)

    accs = tuple(jnp.zeros((8, LANES), F32) for _ in mates)
    if plan.returns <= 16:
        for j in range(plan.returns):
            accs = collect(j, accs)
    else:
        accs = lax.fori_loop(0, plan.returns, collect, accs)

    settle(sums.at[pl.ds(0, total - 1)], sum_recv.at[0])

    def reduce_sums():
        def piece_of(d):
            v = sums[d]
            return v, pltpu.roll(v, LANES - 8, 1)

        if total <= 32:
            level = [piece_of(d) for d in range(total)]
            while len(level) > 1:
                nxt = [add_pair(level[a], level[a + 1]) for a in range(0, len(level) - 1, 2)]
                level = nxt + ([level[-1]] if len(level) % 2 else [])
            return level[0]
        zero = jnp.zeros((1, LANES), F32)
        return lax.fori_loop(0, total, lambda d, a: add_pair(a, piece_of(d)), (zero, zero))

    gram_high, gram_low = reduce_sums()
    gram_high, gram_low = two_sum(gram_high, gram_low)
    real = lax.rem(lax.broadcasted_iota(jnp.int32, (1, LANES), 1), 32) < 8
    gram_high = jnp.broadcast_to(jnp.where(real, gram_high, 0.0), (8, LANES))
    gram_low = jnp.broadcast_to(jnp.where(real, gram_low, 0.0), (8, LANES))

    def entry(i, j):
        s = place(PRODUCTS.index((min(i, j), max(i, j))))
        return pltpu.roll(gram_high, LANES - s, 1) if s else gram_high

    first_gram = [
        [HALF_WIDTH * entry(i, j + 1) + CHAIN[j] * entry(i, j) for j in range(3)]
        for i in range(3)
    ]
    c = solve_small(first_gram, [entry(i, 0) for i in range(3)])
    c = [jnp.broadcast_to(v[:, 0:1], (8, LANES)) for v in c]

    def affine(load_at):
        return ((load_at(0) + c_now[0] * load_at(1)) + c_now[1] * load_at(2)) + c_now[2] * load_at(3)

    c_now = c
    done = []
    for v in range(2):
        side = [
            affine(lambda a, s=s: const[pl.ds((4 * s + a) * 16 + 8 * v, 8), :]) for s in range(4)
        ]
        weight = add_pair(two_product(side[0], side[3]), two_product(side[1], side[2]))
        high_part, low_part = two_product(gram_high, weight[0])
        pair = (high_part, low_part + (gram_high * weight[1] + gram_low * weight[0]))
        for s in (64, 32, 4, 2, 1):
            pair = add_pair(pair, [pltpu.roll(u, LANES - s, 1) for u in pair])
        done.append(pair[0] + pair[1])

    def form(f):
        return jnp.broadcast_to(done[f // 8][f % 8 : f % 8 + 1], (8, LANES))

    d = solve_small([[form(3 * i + j) for j in range(3)] for i in range(3)], [form(9 + i) for i in range(3)])
    d = [jnp.broadcast_to(v[0:1, 0:1], (1, LANES)) for v in d]
    c_now = [v[0:1] for v in c]
    tail = 16 * 16
    coef = affine(lambda a: const[pl.ds(tail + a, 1), :])
    for j in range(3):
        coef = coef + d[j] * affine(lambda a: const[pl.ds(tail + 4 + 4 * j + a, 1), :])

    def spread_coef(k):
        return jnp.broadcast_to(coef[:, k : k + 1], (8, LANES))

    for slot in range(2):
        w = [spread_coef(16 * slot + k) for k in range(7)]
        duo = [jnp.where(row < sy, w[k + 1], w[k + 2]) for k in range(0, 6, 2)]
        for cc in range(3):
            for i in range(sx):
                v = None
                for k in range(0, 6, 2):
                    u = duo[k // 2] * accs[mates.index((k, cc, i))]
                    v = u if v is None else v + u
                start_part = raw[3 + cc, i] * raw[7, i]
                out_ref[slot, cc, i] = w[0][0:sy] * start_part + (v[0:sy] + v[sy : 2 * sy])

    loop(plan.sends, lambda j: piece(j, False))
    loop(n, lambda q: give(q, False))
    settle(sums.at[pl.ds(0, total - 1)], sum_send.at[0])


def per_device(displacement, load, material, free_node, table):
    shard = displacement.shape[1:]
    sx, sy, sz = shard
    grid = tuple(lax.axis_size(a) for a in ("gx", "gy", "gz"))
    plan = Plan(grid, shard)
    ngx, ngy, ngz = grid
    ny = ngy * sy
    groups = plan.groups
    const = jnp.asarray(tables())
    buffers = [
        pltpu.VMEM((FIELDS, sx, sy, sz), F32),
        pltpu.VMEM((2, sx, sy, sz), jnp.int32),
        pltpu.VMEM((plan.sends, plan.tiles, sy, LANES), F32),
        pltpu.VMEM((2, plan.tiles, ngx, ngy, sy, LANES), F32),
        pltpu.VMEM((7, 3, groups, ny, LANES), F32),
        pltpu.VMEM((3, groups, ny, LANES), F32),
        pltpu.VMEM((17, groups, ny, LANES), F32),
        pltpu.VMEM((2, 7, 3 * groups * ny // 8, 8, LANES), F32),
        pltpu.VMEM((ngx, ngy, 6, sy, LANES), F32),
        pltpu.VMEM((plan.returns, 6, sy, LANES), F32),
        pltpu.VMEM((plan.n * ngz, 1, LANES), F32),
        pltpu.VMEM(const.shape, F32),
        pltpu.SMEM(table.shape[::-1], F32),
        pltpu.SemaphoreType.DMA((6,)),
        pltpu.SemaphoreType.DMA((1,)),
        pltpu.SemaphoreType.DMA((2,)),
        pltpu.SemaphoreType.DMA((1,)),
        pltpu.SemaphoreType.DMA((1,)),
        pltpu.SemaphoreType.DMA((1,)),
        pltpu.SemaphoreType.DMA((1,)),
    ]
    operands = (displacement, load, material, free_node, table.T, const)
    both = pl.pallas_call(
        functools.partial(kernel, plan),
        out_shape=jax.ShapeDtypeStruct((2,) + displacement.shape, F32),
        in_specs=[pl.BlockSpec(memory_space=pltpu.HBM)] * 6,
        out_specs=pl.BlockSpec(memory_space=pltpu.VMEM),
        scratch_shapes=buffers,
        compiler_params=pltpu.CompilerParams(
            collective_id=0, has_side_effects=True, vmem_limit_bytes=32 << 20
        ),
    )(*(pltpu.with_memory_space_constraint(a, pltpu.HBM) for a in operands))
    return both[0], both[1]


def solution(mesh):
    in_specs = (
        P(None, "gx", "gy", "gz"),
        P(None, "gx", "gy", "gz"),
        P("gx", "gy", "gz"),
        P("gx", "gy", "gz"),
        P(),
    )
    out_specs = (P(None, "gx", "gy", "gz"), P(None, "gx", "gy", "gz"))
    return jax.shard_map(
        per_device, mesh=mesh, in_specs=in_specs, out_specs=out_specs, check_vma=False
    )
```

time: 23.5 us -> 19.5 us (0.83)
  Pallas kernels: 21.2 us -> 18 us
  local copies, waits for them, and re-layouts: 1.33 us -> 0.61 us
    pallas_call x1, Pallas kernels: 21.2 us -> 18 us  [per_device(): pl.pallas_call(functools.partial(kernel, plan), out_shape=jax.ShapeDtypeS...]
    squeeze x1, local copies, waits for them, and re-layouts: 1.33 us -> 0.61 us  [per_device(): return (both[0], both[1])]
where the time goes in v1:
time: 19.5 us; the launch traced here: 19.2 us
  Pallas kernels  18 us (92%)
  between operations  0.64 us (3%)
  local copies, waits for them, and re-layouts  0.61 us (3%)
    pallas_call x1, Pallas kernels, per_device(): pl.pallas_call(functools.partial(kernel, plan), out_shape=jax.ShapeDtypeS...  18 us
    squeeze x1, local copies, waits for them, and re-layouts, per_device(): return (both[0], both[1])  0.61 us

profile of v1, /device:TPU:0, one launch (start us, length us, event | category | flops | bytes accessed | tf_op | source)
XLA Modules:
  0.0 19.2 jit_solution(16953057290638518848)
XLA Ops:
  0.6 18.0 %shard_map.77 = f32[2,3,2,4,128]{4,3,2,1,0:T(4,128)S(1)} custom-call(f32[3,2,4,128]{3,2,1,0:T(4,128)} %disp_hbm.1, f32[3,2,4,128]{3,2,1,0:T(4,128)} %load_hbm.1, s32[2,4,128]{2,1,0:T(4,128)} %mat_hbm.1, s32[2,4,128]{2,1,0:T(4,128)} %free_hbm.1, f32[3,8]{1,0:T(4,128)} %bitcast.5, f32[272,128]{1,0:T(8,128)} %constant.2.clone.const_hbm), custom_call_target="tpu_custom_call" | custom-call | tf_op jit(solution)/shard_map/pallas_call | solution.py:726
  18.6 0.6 %slice_bitcast_fusion = (f32[3,2,4,128]{3,2,1,0:T(4,128)}, f32[3,2,4,128]{3,2,1,0:T(4,128)}) fusion(f32[2,3,2,4,128]{4,3,2,1,0:T(4,128)S(1)} %shard_map.77), kind=kLoop, calls=%fused_computation | loop fusion | bytes 49152 | tf_op jit(solution)/shard_map/squeeze | solution.py:736

commit v2 on v1

v2 whole, which is shorter than its diff:
```python
import functools

import jax
import jax.numpy as jnp
import numpy as np
from jax import lax
from jax.experimental import pallas as pl
from jax.experimental.pallas import tpu as pltpu
from jax.sharding import PartitionSpec as P

SHIFTS = (9.6, 51.4)
HALF_WIDTH = 29.5
CHAIN = SHIFTS + (30.5,) + SHIFTS + (30.5,)
STEPS = 6
FIELDS = 8
LANES = 128
PRODUCTS = [(i, j) for i in range(7) for j in range(i, 7) if i < 6]
F32 = jnp.float32


def place(t):
    return 32 * (t // 8) + t % 8


def bits(x):
    top = np.asarray(x, np.float32)
    t = np.float32(4097.0) * top
    high = t - (t - top)
    return high, top - high, (x - top.astype(np.float64)).astype(np.float32)


def tables():
    width = 1.0 / np.float64(np.float32(1.0 / HALF_WIDTH))
    chain = np.array([np.float64(np.float32(x / HALF_WIDTH)) * width for x in CHAIN] + [0.0])

    def shifted(x):
        return np.concatenate([[0.0], x[:-1]])

    def times(x):
        return chain * x + width * shifted(x)

    unit = np.eye(7)
    b = [[unit[0]] + [-times(unit[j]) for j in range(3)]]
    for j in range(2):
        b.append([(times(x) - SHIFTS[j] * x) / HALF_WIDTH for x in b[j]])
    forms = [(i, j) for i in range(3) for j in range(3)] + [(i, None) for i in range(3)]
    wide = np.zeros((6, 4, 16, LANES))
    turn = np.zeros((3, 16, LANES))
    for f, (i, j) in enumerate(forms):
        for t, (one, two) in enumerate(PRODUCTS):
            at = place(t)
            turn[:, f, at] = (1.0, 1.0, 0.0) if j is None else (chain[one], chain[two], width)
            for a in range(4):
                left, right = b[i][a], b[j or 0][a]
                wide[0, a, f, at] = left[one]
                wide[1, a, f, at] = left[two] if one != two else 0.0
                wide[2, a, f, at] = right[one]
                wide[3, a, f, at] = right[two]
                wide[4, a, f, at] = shifted(right)[one]
                wide[5, a, f, at] = shifted(right)[two]
    last = np.zeros((2, 4, 8, LANES))
    final = np.zeros((2, 8, LANES))
    for k in range(7):
        final[:, :3, k] = np.array([[chain[k]], [width]])
        final[0, :3, 32 + k] = 1.0
        final[0, 3, k] = final[0, 3, 32 + k] = 1.0
        for a in range(4):
            for j in range(3):
                last[0, a, j, k] = last[0, a, j, 32 + k] = b[j][a][k]
                last[1, a, j, k] = shifted(b[j][a])[k]
            last[0, a, 3, k] = b[0][a][k]
            last[0, a, 3, 32 + k] = -1.0 if 0 < a == k + 1 else 0.0
    blocks = [wide, *(np.stack(bits(x)) for x in turn), last, *(np.stack(bits(x)) for x in final)]
    return np.concatenate([x.reshape(-1, LANES).astype(np.float32) for x in blocks])


def solve_small(gram, right):
    sym = [[0.5 * (gram[i][j] + gram[j][i]) for j in range(3)] for i in range(3)]
    l00 = jnp.sqrt(sym[0][0])
    l10 = sym[1][0] / l00
    l20 = sym[2][0] / l00
    l11 = jnp.sqrt(sym[1][1] - l10 * l10)
    l21 = (sym[2][1] - l20 * l10) / l11
    l22 = jnp.sqrt(sym[2][2] - l20 * l20 - l21 * l21)
    y0 = right[0] / l00
    y1 = (right[1] - l10 * y0) / l11
    y2 = (right[2] - l20 * y0 - l21 * y1) / l22
    c2 = y2 / l22
    c1 = (y1 - l21 * c2) / l11
    c0 = (y0 - l10 * c1 - l20 * c2) / l00
    return [c0, c1, c2]


def two_sum(a, b):
    s = a + b
    t = s - a
    return s, (a - (s - t)) + (b - t)


def add_pair(p, q):
    s, e = two_sum(p[0], q[0])
    return s, e + (p[1] + q[1])


def split(a):
    t = 4097.0 * a
    high = t - (t - a)
    return high, a - high


def two_product(a, b):
    p = a * b
    (ah, al), (bh, bl) = split(a), split(b)
    return p, ((ah * bh - p) + ah * bl + al * bh) + al * bl


def loop(count, body):
    if count <= 32:
        for i in range(count):
            body(i)
    else:

        def step(i, carry):
            body(i)
            return carry

        lax.fori_loop(0, count, step, 0)


def when(condition, body):
    if isinstance(condition, bool):
        if condition:
            body()
    else:
        pl.when(condition)(body)


class Plan:
    def __init__(self, grid, shard):
        self.grid, self.shard = grid, shard
        ngx, ngy, ngz = grid
        sx, sy, sz = shard
        self.n = ngx * ngy
        self.nz = ngz * sz
        self.halo = STEPS
        total = self.n * ngz
        self.pitch = 1 << (-(-self.nz // total) + 2 * self.halo - 1).bit_length()
        spare = total - -(-self.nz // (self.pitch - 2 * self.halo))
        self.counts = [self.n] * (ngz - 1) + [max(2, self.n - spare)]
        self.own = -(-self.nz // sum(self.counts))
        self.span = self.own + 2 * self.halo
        self.hops = [q // ngy + q % ngy // 2 for q in range(self.n)]
        far = max(self.hops) + ngz
        self.within = [sum(h + z <= k for h in self.hops for z in range(ngz)) for k in range(far)]
        self.packed = LANES // self.pitch
        self.groups = ngx * sx // self.packed
        self.mixed = LANES // (sx * self.pitch)
        self.tiles = FIELDS // self.mixed
        self.stride = LANES // (3 * sx)
        self.workers = -(-self.nz // self.own)
        self.base = [sum(self.counts[:z]) for z in range(ngz)]
        own, halo = self.own, self.halo
        self.to_low = [max(0, (sz * z - own - halo) // own + 1) for z in range(ngz)]
        self.to_high = [
            min(self.workers - 1, -(-(sz * z + sz + halo) // own) - 1) for z in range(ngz)
        ]
        self.from_low = [sz * z // own for z in range(ngz)]
        self.from_high = [(sz * z + sz - 1) // own for z in range(ngz)]
        self.sends = max(b - a + 1 for a, b in zip(self.to_low, self.to_high))
        self.returns = max(b - a + 1 for a, b in zip(self.from_low, self.from_high))
        assert sz == LANES and 8 == 2 * sy and own <= self.stride and LANES % self.pitch == 0


def pick(values, z):
    if all(v == values[0] for v in values):
        return values[0]
    out = values[0]
    for k in range(1, len(values)):
        out = jnp.where(z >= k, values[k], out)
    return out


def kernel(
    plan,
    disp_hbm,
    load_hbm,
    mat_hbm,
    free_hbm,
    table_hbm,
    const_hbm,
    out_ref,
    raw,
    flags,
    pack,
    recv,
    basis,
    fields,
    state,
    parts,
    back,
    vt,
    sums,
    const,
    table_ref,
    in_sem,
    send_sem,
    recv_sem,
    back_send,
    back_recv,
    sum_send,
    sum_recv,
    entered,
):
    ngx, ngy, ngz = plan.grid
    sx, sy, sz = plan.shard
    n, own, halo, pitch = plan.n, plan.own, plan.halo, plan.pitch
    nx, ny = ngx * sx, ngy * sy
    groups, mixed, tiles = plan.groups, plan.mixed, plan.tiles
    total = n * ngz
    gx, gy, gz = lax.axis_index("gx"), lax.axis_index("gy"), lax.axis_index("gz")
    p = gx * ngy + gy
    me = p * ngz + gz
    count = pick(plan.counts, gz)
    worker = pick(plan.base, gz) + count - 1 - p
    is_worker = (p < count) & (worker < plan.workers)
    first = own * worker - halo
    settled = jnp.maximum(first, 0)
    low_slab = jnp.minimum(lax.div(settled, sz), ngz - 1)
    edge = sz * (low_slab + 1)
    two = (first + plan.span > edge) & (low_slab + 1 < ngz)
    my_hops = pick(plan.hops, p) + gz

    fetched = [
        pltpu.make_async_copy(disp_hbm, raw.at[pl.ds(0, 3)], in_sem.at[0]),
        pltpu.make_async_copy(load_hbm, raw.at[pl.ds(3, 3)], in_sem.at[1]),
        pltpu.make_async_copy(mat_hbm, flags.at[0], in_sem.at[2]),
        pltpu.make_async_copy(free_hbm, flags.at[1], in_sem.at[3]),
        pltpu.make_async_copy(table_hbm, table_ref, in_sem.at[4]),
        pltpu.make_async_copy(const_hbm, const, in_sem.at[5]),
    ]
    for copy in fetched:
        copy.start()

    def where_is(d):
        return dict(device_id=d, device_id_type=pl.DeviceIdType.LOGICAL)

    def hops_of(d):
        q, z = d // ngz, d % ngz
        return q // ngy + q % ngy // 2 + z

    barrier = pltpu.get_barrier_semaphore()

    def greet(d):
        pl.semaphore_signal(barrier, inc=1, **where_is(d))

    def greet_slab(z):
        def one(q):
            d = q * ngz + z
            when(pick(plan.hops, q) + z < my_hops, lambda: greet(d))

        loop(n, one)

    when(is_worker, lambda: greet_slab(low_slab))
    when(is_worker & two, lambda: greet_slab(low_slab + 1))
    loop(total, lambda d: when((hops_of(d) >= my_hops) & (me != d), lambda: greet(d)))

    for copy in fetched[:4]:
        copy.wait()
    raw[6] = flags[0].astype(F32)
    raw[7] = flags[1].astype(F32)

    lane = lax.broadcasted_iota(jnp.int32, (8, LANES), 1)
    row = lax.broadcasted_iota(jnp.int32, (8, LANES), 0)
    per = 8 // sy
    stacks = -(-tiles // per)
    held = []
    for t in range(stacks):
        part = []
        for e in range(mixed * sx):
            f, i = e // sx, e % sx
            rows = [raw[mixed * min(per * t + h, tiles - 1) + f, i] for h in range(per)]
            part.append(jnp.concatenate(rows, axis=0))
        held.append(part)

    to_low = pick(plan.to_low, gz)
    to_count = pick([b - a + 1 for a, b in zip(plan.to_low, plan.to_high)], gz)

    def route(j):
        w = to_low + j
        z = 0
        for k in range(1, ngz):
            z = z + jnp.where(w >= plan.base[k], 1, 0)
        q = pick([b + c - 1 for b, c in zip(plan.base, plan.counts)], z) - w
        slot = jnp.where(sz * gz > jnp.maximum(own * w - halo, 0), 1, 0)
        return j < to_count, slot, q * ngz + z, pick(plan.hops, q) + z

    def prepare(j):
        w = to_low + j
        offset = sz * gz - (own * w - halo)
        for t in range(stacks):
            out = None
            for e, v in enumerate(held[t]):
                moved = pltpu.roll(v, lax.rem(offset + (pitch * e + 8 * LANES), LANES), 1)
                out = moved if out is None else jnp.where(lane >= pitch * e, moved, out)
            for h in range(min(per, tiles - per * t)):
                pack[j, per * t + h] = out[sy * h : sy * (h + 1)]

    loop(plan.sends, prepare)

    expected = pick(plan.within, my_hops) - 1
    if plan.sends <= 32:
        routes = [route(j) for j in range(plan.sends)]
        for valid, _, _, hops in routes:
            expected = expected + jnp.where(valid & (hops > my_hops), 1, 0)
    else:
        routes = None

        def count_late(j, late):
            valid, _, _, hops = route(j)
            return late + jnp.where(valid & (hops > my_hops), 1, 0)

        expected = lax.fori_loop(0, plan.sends, count_late, expected)
    pl.semaphore_wait(barrier, expected)

    def piece(j, start):
        valid, slot, d, _ = routes[j] if routes else route(j)
        dst = recv.at[slot, :, gx, gy]
        remote = pltpu.make_async_remote_copy(
            src_ref=pack.at[j],
            dst_ref=dst,
            send_sem=send_sem.at[0],
            recv_sem=recv_sem.at[slot],
            **where_is(d),
        )
        if start:
            when(valid & (d != me), remote.start)
            when(
                valid & (d == me),
                lambda: pltpu.make_async_copy(pack.at[j], dst, recv_sem.at[slot]).start(),
            )
        else:
            when(valid & (d != me), remote.wait_send)

    loop(plan.sends, lambda j: piece(j, True))
    loop(
        total,
        lambda d: when(
            hops_of(d) < my_hops,
            lambda: pl.semaphore_signal(entered, inc=1, **where_is(d)),
        ),
    )

    def settle(ref, sem):
        pltpu.make_async_copy(ref, ref, sem).wait()

    def work():
        settle(recv.at[0], recv_sem.at[0])
        when(two, lambda: settle(recv.at[1], recv_sem.at[1]))

        wide_lane = lax.broadcasted_iota(jnp.int32, (ny, LANES), 1)
        depth = lax.rem(wide_lane, pitch)
        plane = depth + first
        near = plane < edge
        seg = sx * pitch

        def gather_rows(slot, k, x):
            return jnp.concatenate([recv[slot, k, x, g] for g in range(ngy)], axis=0)

        def source(k, x):
            return jnp.where(near, gather_rows(0, k, x), gather_rows(1, k, x))

        def unpack(k, g):
            parts_in = [source(k, g * mixed + d) for d in range(mixed)]
            out = []
            for f in range(mixed):
                v = None
                for d in range(mixed):
                    s = (d - f) * seg % LANES
                    moved = pltpu.roll(parts_in[d], s, 1) if s else parts_in[d]
                    v = moved if v is None else jnp.where(wide_lane >= d * seg, moved, v)
                out.append(v)
            return out

        got = [[None] * groups for _ in range(FIELDS)]
        for g in range(groups):
            for k in range(tiles):
                for f, v in enumerate(unpack(k, g)):
                    got[mixed * k + f][g] = v

        span = range(groups)

        def next_z(a):
            return [pltpu.roll(v, LANES - 1, 1) for v in a]

        def last_z(a):
            return [pltpu.roll(v, 1, 1) for v in a]

        def next_y(a):
            return [pltpu.roll(v, ny - 1, 0) for v in a]

        def last_y(a):
            return [pltpu.roll(v, 1, 0) for v in a]

        def next_x(a):
            moved = [pltpu.roll(v, LANES - pitch, 1) for v in a]
            if groups == 1:
                return moved
            return [
                jnp.where(wide_lane >= LANES - pitch, moved[min(g + 1, groups - 1)], moved[g])
                for g in span
            ]

        def last_x(a):
            moved = [pltpu.roll(v, pitch, 1) for v in a]
            if groups == 1:
                return moved
            return [jnp.where(wide_lane < pitch, moved[max(g - 1, 0)], moved[g]) for g in span]

        def both(op, *lists):
            return [op(*vs) for vs in zip(*lists)]

        add = functools.partial(both, lambda a, b: a + b)
        sub = functools.partial(both, lambda a, b: a - b)

        def gradient(vector):
            grad = []
            for v in vector:
                moved = next_z(v)
                total_z, change = add(v, moved), sub(moved, v)
                shifted = next_y(total_z)
                flat, tilt, rise = add(total_z, shifted), sub(shifted, total_z), add(change, next_y(change))
                grad.append(
                    [sub(next_x(flat), flat), add(next_x(tilt), tilt), add(next_x(rise), rise)]
                )
            return grad

        pairs = [(0, 0), (0, 1), (0, 2), (1, 1), (1, 2), (2, 2)]
        free = got[7]
        for c in range(3):
            for g in span:
                basis[0, c, g] = got[3 + c][g] * free[g]
        grad = gradient([got[0], got[1], got[2]])
        mass = []
        high = lax.broadcasted_iota(jnp.int32, (ny, LANES), 0)
        for g in span:
            valid = (high <= ny - 2) & (plane >= 0) & (plane <= plan.nz - 2) & (depth <= plan.span - 2)
            valid = valid & (lax.div(wide_lane, pitch) + g * plan.packed <= nx - 2)
            material = got[6][g]
            zero = jnp.zeros((ny, LANES), F32)
            lame, shear, heavy = zero, zero, zero
            for r in range(table_ref.shape[1]):
                hit = material == float(r)
                lame = jnp.where(hit, table_ref[0, r], lame)
                shear = jnp.where(hit, table_ref[1, r], shear)
                heavy = jnp.where(hit, table_ref[2, r], heavy)
            lame = jnp.where(valid, lame * 0.0625, 0.0)
            shear = jnp.where(valid, shear * 0.0625, 0.0)
            mass.append(jnp.where(valid, heavy * 0.125, 0.0))
            frame = [
                [0.25 * grad[i][j][g] + (1.0 if i == j else 0.0) for j in range(3)] for i in range(3)
            ]
            strain = {}
            for i, j in pairs:
                v = sum(frame[k][i] * frame[k][j] for k in range(3))
                strain[i, j] = 0.5 * (v - 1.0 if i == j else v)
            bulk = lame * (strain[0, 0] + strain[1, 1] + strain[2, 2])
            for i in range(3):
                for j in range(3):
                    state[3 * i + j, g] = frame[i][j]
            for spot, (i, j) in enumerate(pairs):
                v = 2.0 * shear * strain[i, j]
                state[9 + spot, g] = v + bulk if i == j else v
            state[15, g] = lame
            state[16, g] = shear
        mass = add(mass, last_x(mass))
        mass = add(mass, last_y(mass))
        mass = add(mass, last_z(mass))
        for g in span:
            fields[0, g] = free[g]
            fields[1, g] = free[g] * (1.0 / HALF_WIDTH)
            fields[2, g] = (free[g] * mass[g] + (1.0 - free[g])) * (1.0 / HALF_WIDTH)

        rows8 = [pl.ds(8 * r, 8) for r in range(ny // 8)]

        def apply(j):
            grad = gradient([[basis[j, c, g] * fields[0, g] for g in span] for c in range(3)])
            pio = [[[[None] * len(rows8) for _ in span] for _ in range(3)] for _ in range(3)]
            for g in span:
                for r, at in enumerate(rows8):
                    d = [[grad[c][q][g][8 * r : 8 * r + 8] for q in range(3)] for c in range(3)]
                    f = [[state[3 * i + k, g, at] for k in range(3)] for i in range(3)]
                    pulled = [
                        [sum(f[k][a] * d[k][b] for k in range(3)) for b in range(3)] for a in range(3)
                    ]
                    lame, shear = state[15, g, at], state[16, g, at]
                    bulk = lame * (pulled[0][0] + pulled[1][1] + pulled[2][2])
                    t, s = {}, {}
                    for spot, (a, b) in enumerate(pairs):
                        v = shear * (pulled[a][b] + pulled[b][a])
                        t[a, b] = t[b, a] = v + bulk if a == b else v
                        s[a, b] = s[b, a] = state[9 + spot, g, at]
                    for i in range(3):
                        for b in range(3):
                            v = sum(f[i][k] * t[k, b] for k in range(3))
                            pio[i][b][g][r] = v + sum(d[i][k] * s[k, b] for k in range(3))
            for c in range(3):
                e = [[jnp.concatenate(pio[c][b][g], axis=0) for g in span] for b in range(3)]
                across = sub(last_x(e[0]), e[0])
                along = add(last_x(e[1]), e[1])
                up = add(last_x(e[2]), e[2])
                flat = add(last_y(add(across, along)), sub(across, along))
                up = add(up, last_y(up))
                out = add(last_z(add(flat, up)), sub(flat, up))
                for g in span:
                    basis[j + 1, c, g] = fields[1, g] * out[g] + (
                        fields[2, g] - CHAIN[j] / HALF_WIDTH
                    ) * basis[j, c, g]

        for j in range(STEPS):
            apply(j)

        mine = (depth >= halo) & (depth < halo + own) & (plane < plan.nz)
        spots = [(c, g, r) for c in range(3) for g in span for r in range(ny // 8)]
        for k in range(7):
            v = [
                jnp.where(mine[8 * r : 8 * r + 8], basis[k, c, g, rows8[r]], 0.0) for c, g, r in spots
            ]
            top = jnp.abs(v[0])
            for u in v[1:]:
                top = jnp.maximum(top, jnp.abs(u))
            grain = top * (32768.0 * max(1, len(v) // 6))
            for s, u in enumerate(v):
                coarse = (u + grain) - grain
                parts[0, k, s] = coarse
                parts[1, k, s] = u - coarse
        pairs_of = {}
        for i in range(6):
            acc = {j: [None, None] for j in range(i, 7)}
            for s in range(len(spots)):
                ch, cl = parts[0, i, s], parts[1, i, s]
                for j in range(i, 7):
                    dh, dl = parts[0, j, s], parts[1, j, s]
                    new = [ch * dh, cl * (dh + ch + dl) if i == j else ch * dl + cl * (dh + dl)]
                    acc[j] = new if s == 0 else [acc[j][0] + new[0], acc[j][1] + new[1]]
            for j in range(i, 7):
                pairs_of[i, j] = acc[j]
        items = [tuple(pairs_of[q]) for q in PRODUCTS]
        blank = (jnp.zeros((8, LANES), F32), jnp.zeros((8, LANES), F32))
        items = items + [blank] * (32 - len(items))

        def merge(a, b, mask, shift, axis):
            size = 8 if axis == 0 else LANES
            first_in, second_in = [], []
            for u, v in zip(a, b):
                if 2 * shift == size:
                    first_in.append(jnp.where(mask, u, v))
                    second_in.append(pltpu.roll(jnp.where(mask, v, u), shift, axis))
                else:
                    first_in.append(jnp.where(mask, u, pltpu.roll(v, shift, axis)))
                    second_in.append(jnp.where(mask, pltpu.roll(u, size - shift, axis), v))
            return add_pair(first_in, second_in)

        tall = []
        for q in range(4):
            it = items[8 * q : 8 * q + 8]
            one = [merge(it[r], it[r + 4], row < 4, 4, 0) for r in range(4)]
            twice = [merge(one[r], one[r + 2], lax.rem(row, 4) < 2, 2, 0) for r in range(2)]
            tall.append(merge(twice[0], twice[1], lax.rem(row, 2) < 1, 1, 0))
        half = [merge(tall[q], tall[q + 2], lane < 64, 64, 1) for q in range(2)]
        whole = merge(half[0], half[1], lax.rem(lane, 64) < 32, 32, 1)
        for s in (16, 8, 4, 2, 1):
            whole = add_pair(whole, [pltpu.roll(u, LANES - s, 1) for u in whole])
        spread = [pltpu.roll(u, 0, 1, stride=1, stride_axis=0) for u in whole]
        keep = lax.rem(lane, 32) == row
        flat = jnp.where(keep, spread[0], 0.0) + pltpu.roll(jnp.where(keep, spread[1], 0.0), 8, 1)
        sums[worker] = jnp.sum(flat, axis=0, keepdims=True)

    fetched[4].wait()
    when(is_worker, work)
    late = total - pick(plan.within, my_hops)
    when(late > 0, lambda: pl.semaphore_wait(entered, late))

    stride = plan.stride

    def share(d):
        when(
            me != d,
            pltpu.make_async_remote_copy(
                src_ref=sums.at[worker],
                dst_ref=sums.at[worker],
                send_sem=sum_send.at[0],
                recv_sem=sum_recv.at[0],
                **where_is(d),
            ).start,
        )

    def give_back():
        loop(total, share)
        wide_lane = lax.broadcasted_iota(jnp.int32, (ny, LANES), 1)
        for k in range(1, 7):
            for x in range(ngx):
                g, d = x // mixed, x % mixed
                out = None
                for c in range(3):
                    for i in range(sx):
                        e = c * sx + i
                        s = (e * stride - ((d * sx + i) * pitch + halo)) % LANES
                        v = basis[k, c, g]
                        moved = pltpu.roll(v, s, 1) if s else v
                        out = moved if out is None else jnp.where(wide_lane >= e * stride, moved, out)
                for y in range(ngy):
                    back[x, y, k - 1] = out[sy * y : sy * (y + 1)]
        loop(n, lambda q: give(q, True))

    own_low = jnp.minimum(lax.div(own * worker, sz), ngz - 1)
    own_high = lax.div(jnp.minimum(own * worker + own, plan.nz) - 1, sz)
    straddles = sz % own != 0

    def give(q, start):
        x, y = (q // ngy, q % ngy) if isinstance(q, int) else (lax.div(q, ngy), lax.rem(q, ngy))

        def to(z):
            d = q * ngz + z
            dst = vt.at[worker - pick(plan.from_low, z)]
            remote = pltpu.make_async_remote_copy(
                src_ref=back.at[x, y],
                dst_ref=dst,
                send_sem=back_send.at[0],
                recv_sem=back_recv.at[0],
                **where_is(d),
            )
            if start:
                when(d != me, remote.start)
                when(
                    d == me,
                    lambda: pltpu.make_async_copy(back.at[x, y], dst, back_recv.at[0]).start(),
                )
            else:
                when(d != me, remote.wait_send)

        to(own_low)
        if straddles:
            when(own_high > own_low, lambda: to(own_high))

    when(is_worker, give_back)
    fetched[5].wait()

    counts = [b - a + 1 for a, b in zip(plan.from_low, plan.from_high)]
    if min(counts) == plan.returns:
        settle(vt, back_recv.at[0])
    else:
        for z in range(ngz):
            when(gz == z, lambda z=z: settle(vt.at[pl.ds(0, counts[z])], back_recv.at[0]))

    mates = [(k, c, i) for k in range(0, 6, 2) for c in range(3) for i in range(sx)]

    def collect(j, accs):
        w = pick(plan.from_low, gz) + j
        offset = own * w - sz * gz
        inside = (lane >= offset) & (lane < offset + own)
        if min(counts) != plan.returns:
            inside = inside & (j < pick(counts, gz))
        new = []
        stacked = [jnp.concatenate([vt[j, k], vt[j, k + 1]], axis=0) for k in range(0, 6, 2)]
        for (k, c, i), acc in zip(mates, accs):
            s = lax.rem(offset - (c * sx + i) * stride + 2 * LANES, LANES)
            moved = pltpu.roll(stacked[k // 2], s, 1)
            new.append(jnp.where(inside, moved, acc))
        return tuple(new)

    accs = tuple(jnp.zeros((8, LANES), F32) for _ in mates)
    if plan.returns <= 16:
        for j in range(plan.returns):
            accs = collect(j, accs)
    else:
        accs = lax.fori_loop(0, plan.returns, collect, accs)

    active = plan.workers
    when(is_worker, lambda: settle(sums.at[pl.ds(0, active - 1)], sum_recv.at[0]))
    when(jnp.logical_not(is_worker), lambda: settle(sums, sum_recv.at[0]))

    def reduce_sums():
        def piece_of(d):
            v = sums[d]
            return v, pltpu.roll(v, LANES - 8, 1)

        if active <= 32:
            level = [piece_of(d) for d in range(active)]
            while len(level) > 1:
                nxt = [add_pair(level[a], level[a + 1]) for a in range(0, len(level) - 1, 2)]
                level = nxt + ([level[-1]] if len(level) % 2 else [])
            return level[0]
        zero = jnp.zeros((1, LANES), F32)
        return lax.fori_loop(0, active, lambda d, a: add_pair(a, piece_of(d)), (zero, zero))

    gram_high, gram_low = reduce_sums()
    gram_high, gram_low = two_sum(gram_high, gram_low)
    real = lax.rem(lax.broadcasted_iota(jnp.int32, (1, LANES), 1), 32) < 8
    gram_high = jnp.broadcast_to(jnp.where(real, gram_high, 0.0), (8, LANES))
    gram_low = jnp.broadcast_to(jnp.where(real, gram_low, 0.0), (8, LANES))

    def entry(i, j):
        s = place(PRODUCTS.index((min(i, j), max(i, j))))
        return pltpu.roll(gram_high, LANES - s, 1) if s else gram_high

    first_gram = [
        [HALF_WIDTH * entry(i, j + 1) + CHAIN[j] * entry(i, j) for j in range(3)]
        for i in range(3)
    ]
    c = solve_small(first_gram, [entry(i, 0) for i in range(3)])
    c = [jnp.broadcast_to(v[:, 0:1], (8, LANES)) for v in c]

    def affine(c, load_at):
        return ((load_at(0) + c[0] * load_at(1)) + c[1] * load_at(2)) + c[2] * load_at(3)

    def scaled(at, size, x):
        ch, cl, rest = (const[pl.ds(q, size), :] for q in at)
        xh, xl = split(x)
        p = (ch + cl) * x
        return p, (((ch * xh - p) + ch * xl + cl * xh) + cl * xl) + rest * x

    done = []
    for v in range(2):
        side = [
            affine(c, lambda a, s=s: const[pl.ds((4 * s + a) * 16 + 8 * v, 8), :])
            for s in range(6)
        ]
        turn = [[24 * 16 + (3 * q + part) * 16 + 8 * v for part in range(3)] for q in range(3)]
        image = [
            add_pair(scaled(turn[q], 8, side[2 + q]), scaled(turn[2], 8, side[4 + q]))
            for q in range(2)
        ]

        def times_pair(x, pair):
            p, e = two_product(x, pair[0])
            return p, e + x * pair[1]

        weight = add_pair(times_pair(side[0], image[1]), times_pair(side[1], image[0]))
        high_part, low_part = two_product(gram_high, weight[0])
        pair = (high_part, low_part + (gram_high * weight[1] + gram_low * weight[0]))
        for s in (64, 32, 4, 2, 1):
            pair = add_pair(pair, [pltpu.roll(u, LANES - s, 1) for u in pair])
        done.append(pair[0] + pair[1])

    def form(f):
        return jnp.broadcast_to(done[f // 8][f % 8 : f % 8 + 1], (8, LANES))

    gram = [[form(3 * i + j) for j in range(3)] for i in range(3)]
    d = solve_small(gram, [form(9 + i) for i in range(3)])
    d = [jnp.broadcast_to(v[:, 0:1], (8, LANES)) for v in d]
    base_at = 24 * 16 + 9 * 16
    vector = affine(c, lambda a: const[pl.ds(base_at + 8 * a, 8), :])
    moved = affine(c, lambda a: const[pl.ds(base_at + 32 + 8 * a, 8), :])
    turn = [[base_at + 64 + 8 * (3 * q + part) for part in range(3)] for q in range(2)]
    image = add_pair(scaled(turn[0], 8, vector), scaled(turn[1], 8, moved))
    factor = jnp.where(row == 0, -d[0], jnp.where(row == 1, -d[1], jnp.where(row == 2, -d[2], 1.0)))
    coef = times_pair(factor, image)
    coef = add_pair(coef, [pltpu.roll(u, 6, 0) for u in coef])
    coef = add_pair(coef, [pltpu.roll(u, 7, 0) for u in coef])
    coef = two_sum(coef[0][0:1], coef[1][0:1])

    def spread_coef(part, k):
        return jnp.broadcast_to(coef[part][:, k : k + 1], (8, LANES))

    for slot in range(2):
        sets = [[-spread_coef(0, 32 + k) for k in range(7)]]
        if slot == 1:
            sets = [[spread_coef(part, k) for k in range(7)] for part in range(2)]
        duo = [
            [jnp.where(row < sy, w[k + 1], w[k + 2]) for w in sets] for k in range(0, 6, 2)
        ]
        for cc in range(3):
            for i in range(sx):
                v = None
                for k in range(0, 6, 2):
                    held_k = accs[mates.index((k, cc, i))]
                    u = duo[k // 2][0] * held_k
                    for extra in duo[k // 2][1:]:
                        u = u + extra * held_k
                    v = u if v is None else v + u
                start_part = raw[3 + cc, i] * raw[7, i]
                head = sets[0][0][0:sy] * start_part
                for extra in sets[1:]:
                    head = head + extra[0][0:sy] * start_part
                out_ref[slot, cc, i] = head + (v[0:sy] + v[sy : 2 * sy])

    loop(plan.sends, lambda j: piece(j, False))

    def sent():
        loop(n, lambda q: give(q, False))
        left = total - 1
        while left:
            rows = min(left, active)
            settle(sums.at[pl.ds(0, rows)], sum_send.at[0])
            left -= rows

    when(is_worker, sent)


def per_device(displacement, load, material, free_node, table):
    shard = displacement.shape[1:]
    sx, sy, sz = shard
    grid = tuple(lax.axis_size(a) for a in ("gx", "gy", "gz"))
    plan = Plan(grid, shard)
    ngx, ngy, ngz = grid
    ny = ngy * sy
    groups = plan.groups
    const = jnp.asarray(tables())
    buffers = [
        pltpu.VMEM((FIELDS, sx, sy, sz), F32),
        pltpu.VMEM((2, sx, sy, sz), jnp.int32),
        pltpu.VMEM((plan.sends, plan.tiles, sy, LANES), F32),
        pltpu.VMEM((2, plan.tiles, ngx, ngy, sy, LANES), F32),
        pltpu.VMEM((7, 3, groups, ny, LANES), F32),
        pltpu.VMEM((3, groups, ny, LANES), F32),
        pltpu.VMEM((17, groups, ny, LANES), F32),
        pltpu.VMEM((2, 7, 3 * groups * ny // 8, 8, LANES), F32),
        pltpu.VMEM((ngx, ngy, 6, sy, LANES), F32),
        pltpu.VMEM((plan.returns, 6, sy, LANES), F32),
        pltpu.VMEM((plan.workers, 1, LANES), F32),
        pltpu.VMEM(const.shape, F32),
        pltpu.SMEM(table.shape[::-1], F32),
        pltpu.SemaphoreType.DMA((6,)),
        pltpu.SemaphoreType.DMA((1,)),
        pltpu.SemaphoreType.DMA((2,)),
        pltpu.SemaphoreType.DMA((1,)),
        pltpu.SemaphoreType.DMA((1,)),
        pltpu.SemaphoreType.DMA((1,)),
        pltpu.SemaphoreType.DMA((1,)),
        pltpu.SemaphoreType.REGULAR,
    ]
    operands = (displacement, load, material, free_node, table.T, const)
    both = pl.pallas_call(
        functools.partial(kernel, plan),
        out_shape=jax.ShapeDtypeStruct((2,) + displacement.shape, F32),
        in_specs=[pl.BlockSpec(memory_space=pltpu.HBM)] * 6,
        out_specs=pl.BlockSpec(memory_space=pltpu.VMEM),
        scratch_shapes=buffers,
        compiler_params=pltpu.CompilerParams(
            collective_id=0, has_side_effects=True, vmem_limit_bytes=32 << 20
        ),
    )(*(pltpu.with_memory_space_constraint(a, pltpu.HBM) for a in operands))
    return both[0], both[1]


def solution(mesh):
    in_specs = (
        P(None, "gx", "gy", "gz"),
        P(None, "gx", "gy", "gz"),
        P("gx", "gy", "gz"),
        P("gx", "gy", "gz"),
        P(),
    )
    out_specs = (P(None, "gx", "gy", "gz"), P(None, "gx", "gy", "gz"))
    return jax.shard_map(
        per_device, mesh=mesh, in_specs=in_specs, out_specs=out_specs, check_vma=False
    )
```

time: 19.5 us -> 17.9 us (0.918)
  Pallas kernels: 18 us -> 16.4 us
    pallas_call x1, Pallas kernels: 18 us -> 16.4 us  [per_device(): pl.pallas_call(functools.partial(kernel, plan), out_shape=jax.ShapeDtypeS...]
where the time goes in v2:
time: 17.9 us; the launch traced here: 17.7 us
  Pallas kernels  16.4 us (92%)
  between operations  0.64 us (4%)
  local copies, waits for them, and re-layouts  0.61 us (3%)
    pallas_call x1, Pallas kernels, per_device(): pl.pallas_call(functools.partial(kernel, plan), out_shape=jax.ShapeDtypeS...  16.4 us
    squeeze x1, local copies, waits for them, and re-layouts, per_device(): return (both[0], both[1])  0.61 us

profile of v2, /device:TPU:0, one launch (start us, length us, event | category | flops | bytes accessed | tf_op | source)
XLA Modules:
  0.0 17.7 jit_solution(1395558116969058268)
XLA Ops:
  0.6 16.4 %shard_map.77 = f32[2,3,2,4,128]{4,3,2,1,0:T(4,128)S(1)} custom-call(f32[3,2,4,128]{3,2,1,0:T(4,128)} %disp_hbm.1, f32[3,2,4,128]{3,2,1,0:T(4,128)} %load_hbm.1, s32[2,4,128]{2,1,0:T(4,128)} %mat_hbm.1, s32[2,4,128]{2,1,0:T(4,128)} %free_hbm.1, f32[3,8]{1,0:T(4,128)} %bitcast.5, f32[640,128]{1,0:T(8,128)} %constant.2.clone.const_hbm), custom_call_target="tpu_custom_call" | custom-call | tf_op jit(solution)/shard_map/pallas_call | solution.py:833
  17.1 0.6 %slice_bitcast_fusion = (f32[3,2,4,128]{3,2,1,0:T(4,128)}, f32[3,2,4,128]{3,2,1,0:T(4,128)}) fusion(f32[2,3,2,4,128]{4,3,2,1,0:T(4,128)S(1)} %shard_map.77), kind=kLoop, calls=%fused_computation | loop fusion | bytes 49152 | tf_op jit(solution)/shard_map/squeeze | solution.py:843

commit v3 on v2

--- a/solution.py
+++ b/solution.py
@@ -19,7 +19,7 @@
 
 
 def place(t):
-    return 32 * (t // 8) + t % 8
+    return 32 * (t // 8) + 8 + t % 8
 
 
 def bits(x):
@@ -76,18 +76,17 @@
 
 def solve_small(gram, right):
     sym = [[0.5 * (gram[i][j] + gram[j][i]) for j in range(3)] for i in range(3)]
-    l00 = jnp.sqrt(sym[0][0])
-    l10 = sym[1][0] / l00
-    l20 = sym[2][0] / l00
-    l11 = jnp.sqrt(sym[1][1] - l10 * l10)
-    l21 = (sym[2][1] - l20 * l10) / l11
-    l22 = jnp.sqrt(sym[2][2] - l20 * l20 - l21 * l21)
-    y0 = right[0] / l00
-    y1 = (right[1] - l10 * y0) / l11
-    y2 = (right[2] - l20 * y0 - l21 * y1) / l22
-    c2 = y2 / l22
-    c1 = (y1 - l21 * c2) / l11
-    c0 = (y0 - l10 * c1 - l20 * c2) / l00
+    r0 = 1.0 / sym[0][0]
+    l10 = sym[1][0] * r0
+    l20 = sym[2][0] * r0
+    r1 = 1.0 / (sym[1][1] - l10 * sym[1][0])
+    e = sym[2][1] - l20 * sym[1][0]
+    l21 = e * r1
+    d2 = sym[2][2] - l20 * sym[2][0] - l21 * e
+    y1 = right[1] - l10 * right[0]
+    c2 = (right[2] - l20 * right[0] - l21 * y1) / d2
+    c1 = y1 * r1 - l21 * c2
+    c0 = right[0] * r0 - l10 * c1 - l20 * c2
     return [c0, c1, c2]
 
 
@@ -100,6 +99,13 @@
 def add_pair(p, q):
     s, e = two_sum(p[0], q[0])
     return s, e + (p[1] + q[1])
+
+
+def add_all(pairs):
+    while len(pairs) > 1:
+        rest = pairs[len(pairs) & ~1 :]
+        pairs = [add_pair(p, q) for p, q in zip(pairs[::2], pairs[1::2])] + rest
+    return pairs[0]
 
 
 def split(a):
@@ -149,9 +155,6 @@
         self.counts = [self.n] * (ngz - 1) + [max(2, self.n - spare)]
         self.own = -(-self.nz // sum(self.counts))
         self.span = self.own + 2 * self.halo
-        self.hops = [q // ngy + q % ngy // 2 for q in range(self.n)]
-        far = max(self.hops) + ngz
-        self.within = [sum(h + z <= k for h in self.hops for z in range(ngz)) for k in range(far)]
         self.packed = LANES // self.pitch
         self.groups = ngx * sx // self.packed
         self.mixed = LANES // (sx * self.pitch)
@@ -228,7 +231,7 @@
     low_slab = jnp.minimum(lax.div(settled, sz), ngz - 1)
     edge = sz * (low_slab + 1)
     two = (first + plan.span > edge) & (low_slab + 1 < ngz)
-    my_hops = pick(plan.hops, p) + gz
+    last = total - 1
 
     fetched = [
         pltpu.make_async_copy(disp_hbm, raw.at[pl.ds(0, 3)], in_sem.at[0]),
@@ -244,10 +247,6 @@
     def where_is(d):
         return dict(device_id=d, device_id_type=pl.DeviceIdType.LOGICAL)
 
-    def hops_of(d):
-        q, z = d // ngz, d % ngz
-        return q // ngy + q % ngy // 2 + z
-
     barrier = pltpu.get_barrier_semaphore()
 
     def greet(d):
@@ -256,13 +255,13 @@
     def greet_slab(z):
         def one(q):
             d = q * ngz + z
-            when(pick(plan.hops, q) + z < my_hops, lambda: greet(d))
+            when((d != me) & (d != last), lambda: greet(d))
 
         loop(n, one)
 
     when(is_worker, lambda: greet_slab(low_slab))
     when(is_worker & two, lambda: greet_slab(low_slab + 1))
-    loop(total, lambda d: when((hops_of(d) >= my_hops) & (me != d), lambda: greet(d)))
+    when(me != last, lambda: greet(last))
 
     for copy in fetched[:4]:
         copy.wait()
@@ -292,7 +291,7 @@
             z = z + jnp.where(w >= plan.base[k], 1, 0)
         q = pick([b + c - 1 for b, c in zip(plan.base, plan.counts)], z) - w
         slot = jnp.where(sz * gz > jnp.maximum(own * w - halo, 0), 1, 0)
-        return j < to_count, slot, q * ngz + z, pick(plan.hops, q) + z
+        return j < to_count, slot, q * ngz + z
 
     def prepare(j):
         w = to_low + j
@@ -307,23 +306,24 @@
 
     loop(plan.sends, prepare)
 
-    expected = pick(plan.within, my_hops) - 1
+    expected = to_count
     if plan.sends <= 32:
         routes = [route(j) for j in range(plan.sends)]
-        for valid, _, _, hops in routes:
-            expected = expected + jnp.where(valid & (hops > my_hops), 1, 0)
+        for valid, _, d in routes:
+            expected = expected - jnp.where(valid & (d == me), 1, 0)
     else:
         routes = None
 
-        def count_late(j, late):
-            valid, _, _, hops = route(j)
-            return late + jnp.where(valid & (hops > my_hops), 1, 0)
-
-        expected = lax.fori_loop(0, plan.sends, count_late, expected)
+        def count_self(j, seen):
+            valid, _, d = route(j)
+            return seen - jnp.where(valid & (d == me), 1, 0)
+
+        expected = lax.fori_loop(0, plan.sends, count_self, expected)
+    expected = jnp.where(me == last, total - 1, expected)
     pl.semaphore_wait(barrier, expected)
 
     def piece(j, start):
-        valid, slot, d, _ = routes[j] if routes else route(j)
+        valid, slot, d = routes[j] if routes else route(j)
         dst = recv.at[slot, :, gx, gy]
         remote = pltpu.make_async_remote_copy(
             src_ref=pack.at[j],
@@ -342,13 +342,11 @@
             when(valid & (d != me), remote.wait_send)
 
     loop(plan.sends, lambda j: piece(j, True))
-    loop(
-        total,
-        lambda d: when(
-            hops_of(d) < my_hops,
-            lambda: pl.semaphore_signal(entered, inc=1, **where_is(d)),
-        ),
-    )
+
+    def announce():
+        loop(total - 1, lambda d: pl.semaphore_signal(entered, inc=1, **where_is(d)))
+
+    when(me == last, announce)
 
     def settle(ref, sem):
         pltpu.make_async_copy(ref, ref, sem).wait()
@@ -389,32 +387,25 @@
 
         span = range(groups)
 
-        def next_z(a):
-            return [pltpu.roll(v, LANES - 1, 1) for v in a]
-
-        def last_z(a):
-            return [pltpu.roll(v, 1, 1) for v in a]
-
         def next_y(a):
             return [pltpu.roll(v, ny - 1, 0) for v in a]
 
         def last_y(a):
             return [pltpu.roll(v, 1, 0) for v in a]
 
-        def next_x(a):
-            moved = [pltpu.roll(v, LANES - pitch, 1) for v in a]
-            if groups == 1:
+        def forward(a, x, z):
+            moved = [pltpu.roll(v, LANES - pitch * x - z, 1) for v in a]
+            if groups == 1 or not x:
                 return moved
-            return [
-                jnp.where(wide_lane >= LANES - pitch, moved[min(g + 1, groups - 1)], moved[g])
-                for g in span
-            ]
-
-        def last_x(a):
-            moved = [pltpu.roll(v, pitch, 1) for v in a]
-            if groups == 1:
+            wrap = wide_lane >= LANES - pitch
+            return [jnp.where(wrap, moved[min(g + 1, groups - 1)], moved[g]) for g in span]
+
+        def backward(a, x, z):
+            moved = [pltpu.roll(v, pitch * x + z, 1) for v in a]
+            if groups == 1 or not x:
                 return moved
-            return [jnp.where(wide_lane < pitch, moved[max(g - 1, 0)], moved[g]) for g in span]
+            wrap = wide_lane < pitch
+            return [jnp.where(wrap, moved[max(g - 1, 0)], moved[g]) for g in span]
 
         def both(op, *lists):
             return [op(*vs) for vs in zip(*lists)]
@@ -425,13 +416,11 @@
         def gradient(vector):
             grad = []
             for v in vector:
-                moved = next_z(v)
-                total_z, change = add(v, moved), sub(moved, v)
-                shifted = next_y(total_z)
-                flat, tilt, rise = add(total_z, shifted), sub(shifted, total_z), add(change, next_y(change))
-                grad.append(
-                    [sub(next_x(flat), flat), add(next_x(tilt), tilt), add(next_x(rise), rise)]
-                )
+                above, over, far = forward(v, 0, 1), forward(v, 1, 0), forward(v, 1, 1)
+                near_z, far_z = add(v, above), add(over, far)
+                wide, flat = sub(far_z, near_z), add(far_z, near_z)
+                rise = add(sub(above, v), sub(far, over))
+                grad.append([add(next_y(wide), wide), sub(next_y(flat), flat), add(next_y(rise), rise)])
             return grad
 
         pairs = [(0, 0), (0, 1), (0, 2), (1, 1), (1, 2), (2, 2)]
@@ -472,9 +461,10 @@
                 state[9 + spot, g] = v + bulk if i == j else v
             state[15, g] = lame
             state[16, g] = shear
-        mass = add(mass, last_x(mass))
         mass = add(mass, last_y(mass))
-        mass = add(mass, last_z(mass))
+        mass = add(
+            add(mass, backward(mass, 0, 1)), add(backward(mass, 1, 0), backward(mass, 1, 1))
+        )
         for g in span:
             fields[0, g] = free[g]
             fields[1, g] = free[g] * (1.0 / HALF_WIDTH)
@@ -505,12 +495,14 @@
                             pio[i][b][g][r] = v + sum(d[i][k] * s[k, b] for k in range(3))
             for c in range(3):
                 e = [[jnp.concatenate(pio[c][b][g], axis=0) for g in span] for b in range(3)]
-                across = sub(last_x(e[0]), e[0])
-                along = add(last_x(e[1]), e[1])
-                up = add(last_x(e[2]), e[2])
-                flat = add(last_y(add(across, along)), sub(across, along))
-                up = add(up, last_y(up))
-                out = add(last_z(add(flat, up)), sub(flat, up))
+                wide = add(e[0], last_y(e[0]))
+                tilt = sub(last_y(e[1]), e[1])
+                rise = add(e[2], last_y(e[2]))
+                minus, plus = sub(tilt, wide), add(tilt, wide)
+                out = add(
+                    add(sub(minus, rise), backward(add(minus, rise), 0, 1)),
+                    add(backward(sub(plus, rise), 1, 0), backward(add(plus, rise), 1, 1)),
+                )
                 for g in span:
                     basis[j + 1, c, g] = fields[1, g] * out[g] + (
                         fields[2, g] - CHAIN[j] / HALF_WIDTH
@@ -566,19 +558,36 @@
             one = [merge(it[r], it[r + 4], row < 4, 4, 0) for r in range(4)]
             twice = [merge(one[r], one[r + 2], lax.rem(row, 4) < 2, 2, 0) for r in range(2)]
             tall.append(merge(twice[0], twice[1], lax.rem(row, 2) < 1, 1, 0))
-        half = [merge(tall[q], tall[q + 2], lane < 64, 64, 1) for q in range(2)]
-        whole = merge(half[0], half[1], lax.rem(lane, 64) < 32, 32, 1)
-        for s in (16, 8, 4, 2, 1):
-            whole = add_pair(whole, [pltpu.roll(u, LANES - s, 1) for u in whole])
-        spread = [pltpu.roll(u, 0, 1, stride=1, stride_axis=0) for u in whole]
-        keep = lax.rem(lane, 32) == row
-        flat = jnp.where(keep, spread[0], 0.0) + pltpu.roll(jnp.where(keep, spread[1], 0.0), 8, 1)
-        sums[worker] = jnp.sum(flat, axis=0, keepdims=True)
+        quarter = lane // 32
+
+        def turned(j):
+            out = []
+            for part in range(2):
+                v = None
+                for q in range(4):
+                    u = tall[q][part]
+                    u = pltpu.roll(u, LANES - 32 * j, 1) if j else u
+                    v = u if v is None else jnp.where(quarter >= q, u, v)
+                out.append(v)
+            return out
+
+        whole = add_all([turned(j) for j in range(4)])
+        whole = add_all(
+            [[pltpu.roll(u, LANES - 8 * j, 1) if j else u for u in whole] for j in range(4)]
+        )
+        whole = add_all(
+            [
+                [pltpu.roll(u, 8 - j, 1, stride=1, stride_axis=0) for u in whole]
+                for j in range(8)
+            ]
+        )
+        keep = lax.rem(lane, 32) == row + 8
+        ends = [jnp.sum(jnp.where(keep, u, 0.0), axis=0, keepdims=True) for u in whole]
+        sums[worker] = jnp.concatenate(ends, axis=0)
 
     fetched[4].wait()
     when(is_worker, work)
-    late = total - pick(plan.within, my_hops)
-    when(late > 0, lambda: pl.semaphore_wait(entered, late))
+    when(me != last, lambda: pl.semaphore_wait(entered, 1))
 
     stride = plan.stride
 
@@ -680,35 +689,27 @@
     when(jnp.logical_not(is_worker), lambda: settle(sums, sum_recv.at[0]))
 
     def reduce_sums():
-        def piece_of(d):
-            v = sums[d]
-            return v, pltpu.roll(v, LANES - 8, 1)
-
+        zero = jnp.zeros((2, LANES), F32)
         if active <= 32:
-            level = [piece_of(d) for d in range(active)]
-            while len(level) > 1:
-                nxt = [add_pair(level[a], level[a + 1]) for a in range(0, len(level) - 1, 2)]
-                level = nxt + ([level[-1]] if len(level) % 2 else [])
-            return level[0]
-        zero = jnp.zeros((1, LANES), F32)
-        return lax.fori_loop(0, active, lambda d, a: add_pair(a, piece_of(d)), (zero, zero))
-
-    gram_high, gram_low = reduce_sums()
-    gram_high, gram_low = two_sum(gram_high, gram_low)
-    real = lax.rem(lax.broadcasted_iota(jnp.int32, (1, LANES), 1), 32) < 8
-    gram_high = jnp.broadcast_to(jnp.where(real, gram_high, 0.0), (8, LANES))
-    gram_low = jnp.broadcast_to(jnp.where(real, gram_low, 0.0), (8, LANES))
+            return add_all([(sums[d], zero) for d in range(active)])
+        return lax.fori_loop(
+            0, active, lambda d, a: add_pair(a, (sums[d], zero)), (zero, zero)
+        )
+
+    raw_sum, lost = reduce_sums()
+    gram_high, gram_low = two_sum(raw_sum[0:1], raw_sum[1:2] + lost[0:1])
+    gram_high = jnp.broadcast_to(gram_high, (8, LANES))
+    gram_low = jnp.broadcast_to(gram_low, (8, LANES))
 
     def entry(i, j):
         s = place(PRODUCTS.index((min(i, j), max(i, j))))
-        return pltpu.roll(gram_high, LANES - s, 1) if s else gram_high
+        return jnp.broadcast_to(gram_high[:, s : s + 1], (8, LANES))
 
     first_gram = [
         [HALF_WIDTH * entry(i, j + 1) + CHAIN[j] * entry(i, j) for j in range(3)]
         for i in range(3)
     ]
     c = solve_small(first_gram, [entry(i, 0) for i in range(3)])
-    c = [jnp.broadcast_to(v[:, 0:1], (8, LANES)) for v in c]
 
     def affine(c, load_at):
         return ((load_at(0) + c[0] * load_at(1)) + c[1] * load_at(2)) + c[2] * load_at(3)
@@ -738,16 +739,17 @@
         weight = add_pair(times_pair(side[0], image[1]), times_pair(side[1], image[0]))
         high_part, low_part = two_product(gram_high, weight[0])
         pair = (high_part, low_part + (gram_high * weight[1] + gram_low * weight[0]))
-        for s in (64, 32, 4, 2, 1):
-            pair = add_pair(pair, [pltpu.roll(u, LANES - s, 1) for u in pair])
-        done.append(pair[0] + pair[1])
+        for s, times in ((32, 4), (1, 8)):
+            pair = add_all(
+                [[pltpu.roll(u, LANES - s * q, 1) if q else u for u in pair] for q in range(times)]
+            )
+        done.append(jnp.broadcast_to((pair[0] + pair[1])[:, 8:9], (8, LANES)))
 
     def form(f):
         return jnp.broadcast_to(done[f // 8][f % 8 : f % 8 + 1], (8, LANES))
 
     gram = [[form(3 * i + j) for j in range(3)] for i in range(3)]
     d = solve_small(gram, [form(9 + i) for i in range(3)])
-    d = [jnp.broadcast_to(v[:, 0:1], (8, LANES)) for v in d]
     base_at = 24 * 16 + 9 * 16
     vector = affine(c, lambda a: const[pl.ds(base_at + 8 * a, 8), :])
     moved = affine(c, lambda a: const[pl.ds(base_at + 32 + 8 * a, 8), :])
@@ -817,7 +819,7 @@
         pltpu.VMEM((2, 7, 3 * groups * ny // 8, 8, LANES), F32),
         pltpu.VMEM((ngx, ngy, 6, sy, LANES), F32),
         pltpu.VMEM((plan.returns, 6, sy, LANES), F32),
-        pltpu.VMEM((plan.workers, 1, LANES), F32),
+        pltpu.VMEM((plan.workers, 2, LANES), F32),
         pltpu.VMEM(const.shape, F32),
         pltpu.SMEM(table.shape[::-1], F32),
         pltpu.SemaphoreType.DMA((6,)),

time: 17.9 us -> 16.3 us (0.911)
  Pallas kernels: 16.4 us -> 14.9 us
    pallas_call x1, Pallas kernels: 16.4 us -> 14.9 us  [per_device(): pl.pallas_call(functools.partial(kernel, plan), out_shape=jax.ShapeDtypeS...]
where the time goes in v3:
time: 16.3 us; the launch traced here: 16.1 us
  Pallas kernels  14.9 us (91%)
  between operations  0.64 us (4%)
  local copies, waits for them, and re-layouts  0.61 us (4%)
    pallas_call x1, Pallas kernels, per_device(): pl.pallas_call(functools.partial(kernel, plan), out_shape=jax.ShapeDtypeS...  14.9 us
    squeeze x1, local copies, waits for them, and re-layouts, per_device(): return (both[0], both[1])  0.61 us

profile of v3, /device:TPU:0, one launch (start us, length us, event | category | flops | bytes accessed | tf_op | source)
XLA Modules:
  0.0 16.1 jit_solution(12361985802406287737)
XLA Ops:
  0.6 14.9 %shard_map.77 = f32[2,3,2,4,128]{4,3,2,1,0:T(4,128)S(1)} custom-call(f32[3,2,4,128]{3,2,1,0:T(4,128)} %disp_hbm.1, f32[3,2,4,128]{3,2,1,0:T(4,128)} %load_hbm.1, s32[2,4,128]{2,1,0:T(4,128)} %mat_hbm.1, s32[2,4,128]{2,1,0:T(4,128)} %free_hbm.1, f32[3,8]{1,0:T(4,128)} %bitcast.5, f32[640,128]{1,0:T(8,128)} %constant.2.clone.const_hbm), custom_call_target="tpu_custom_call" | custom-call | tf_op jit(solution)/shard_map/pallas_call | solution.py:835
  15.5 0.6 %slice_bitcast_fusion = (f32[3,2,4,128]{3,2,1,0:T(4,128)}, f32[3,2,4,128]{3,2,1,0:T(4,128)}) fusion(f32[2,3,2,4,128]{4,3,2,1,0:T(4,128)S(1)} %shard_map.77), kind=kLoop, calls=%fused_computation | loop fusion | bytes 49152 | tf_op jit(solution)/shard_map/squeeze | solution.py:845

commit v4 on v3

--- a/solution.py
+++ b/solution.py
@@ -13,8 +13,11 @@
 CHAIN = SHIFTS + (30.5,) + SHIFTS + (30.5,)
 STEPS = 6
 FIELDS = 8
+ORDER = (0, 3, 1, 4, 2, 5, 6, 7)
 LANES = 128
-PRODUCTS = [(i, j) for i in range(7) for j in range(i, 7) if i < 6]
+PRODUCTS = {(i, j): t for t, (i, j) in enumerate((i, j) for i in range(6) for j in range(i, 6))}
+PRODUCTS.update({(i, 6): 24 + i for i in range(6)})
+EARLY = {(i, j): t for t, (i, j) in enumerate((i, j) for i in range(3) for j in range(i, 4))}
 F32 = jnp.float32
 
 
@@ -47,7 +50,7 @@
     wide = np.zeros((6, 4, 16, LANES))
     turn = np.zeros((3, 16, LANES))
     for f, (i, j) in enumerate(forms):
-        for t, (one, two) in enumerate(PRODUCTS):
+        for (one, two), t in PRODUCTS.items():
             at = place(t)
             turn[:, f, at] = (1.0, 1.0, 0.0) if j is None else (chain[one], chain[two], width)
             for a in range(4):
@@ -101,11 +104,15 @@
     return s, e + (p[1] + q[1])
 
 
-def add_all(pairs):
-    while len(pairs) > 1:
-        rest = pairs[len(pairs) & ~1 :]
-        pairs = [add_pair(p, q) for p, q in zip(pairs[::2], pairs[1::2])] + rest
-    return pairs[0]
+def add_parts(p, q):
+    return add_pair(p, q) if len(p) == 2 else (p[0] + q[0],)
+
+
+def add_all(terms):
+    while len(terms) > 1:
+        rest = terms[len(terms) & ~1 :]
+        terms = [add_parts(p, q) for p, q in zip(terms[::2], terms[1::2])] + rest
+    return terms[0]
 
 
 def split(a):
@@ -202,7 +209,9 @@
     parts,
     back,
     vt,
+    first_sums,
     sums,
+    talls,
     const,
     table_ref,
     in_sem,
@@ -277,9 +286,17 @@
         part = []
         for e in range(mixed * sx):
             f, i = e // sx, e % sx
-            rows = [raw[mixed * min(per * t + h, tiles - 1) + f, i] for h in range(per)]
+            rows = [
+                raw[ORDER[mixed * min(per * t + h, tiles - 1) + f], i] for h in range(per)
+            ]
             part.append(jnp.concatenate(rows, axis=0))
-        held.append(part)
+        turned = []
+        for e in range(mixed * sx):
+            v = part[e]
+            for k in range(1, mixed):
+                v = jnp.where(lax.rem(gx, mixed) == k, part[(e - k * sx) % (mixed * sx)], v)
+            turned.append(v)
+        held.append(turned)
 
     to_low = pick(plan.to_low, gz)
     to_count = pick([b - a + 1 for a, b in zip(plan.to_low, plan.to_high)], gz)
@@ -351,6 +368,18 @@
     def settle(ref, sem):
         pltpu.make_async_copy(ref, ref, sem).wait()
 
+    def share(ref, slot, d):
+        when(
+            me != d,
+            pltpu.make_async_remote_copy(
+                src_ref=ref.at[worker],
+                dst_ref=ref.at[worker],
+                send_sem=sum_send.at[slot],
+                recv_sem=sum_recv.at[slot],
+                **where_is(d),
+            ).start,
+        )
+
     def work():
         settle(recv.at[0], recv_sem.at[0])
         when(two, lambda: settle(recv.at[1], recv_sem.at[1]))
@@ -372,18 +401,17 @@
             out = []
             for f in range(mixed):
                 v = None
-                for d in range(mixed):
-                    s = (d - f) * seg % LANES
-                    moved = pltpu.roll(parts_in[d], s, 1) if s else parts_in[d]
-                    v = moved if v is None else jnp.where(wide_lane >= d * seg, moved, v)
-                out.append(v)
+                for at in range(mixed):
+                    u = parts_in[(at - f) % mixed]
+                    v = u if v is None else jnp.where(wide_lane >= at * seg, u, v)
+                out.append(pltpu.roll(v, LANES - f * seg, 1) if f else v)
             return out
 
         got = [[None] * groups for _ in range(FIELDS)]
         for g in range(groups):
             for k in range(tiles):
                 for f, v in enumerate(unpack(k, g)):
-                    got[mixed * k + f][g] = v
+                    got[ORDER[mixed * k + f]][g] = v
 
         span = range(groups)
 
@@ -508,15 +536,12 @@
                         fields[2, g] - CHAIN[j] / HALF_WIDTH
                     ) * basis[j, c, g]
 
-        for j in range(STEPS):
-            apply(j)
-
         mine = (depth >= halo) & (depth < halo + own) & (plane < plan.nz)
         spots = [(c, g, r) for c in range(3) for g in span for r in range(ny // 8)]
-        for k in range(7):
-            v = [
-                jnp.where(mine[8 * r : 8 * r + 8], basis[k, c, g, rows8[r]], 0.0) for c, g, r in spots
-            ]
+        mine = [mine[8 * r : 8 * r + 8] for r in range(ny // 8)]
+
+        def divide(k):
+            v = [jnp.where(mine[r], basis[k, c, g, rows8[r]], 0.0) for c, g, r in spots]
             top = jnp.abs(v[0])
             for u in v[1:]:
                 top = jnp.maximum(top, jnp.abs(u))
@@ -525,86 +550,105 @@
                 coarse = (u + grain) - grain
                 parts[0, k, s] = coarse
                 parts[1, k, s] = u - coarse
-        pairs_of = {}
-        for i in range(6):
-            acc = {j: [None, None] for j in range(i, 7)}
+
+        def products(i, js):
+            acc = {}
             for s in range(len(spots)):
                 ch, cl = parts[0, i, s], parts[1, i, s]
-                for j in range(i, 7):
+                for j in js:
                     dh, dl = parts[0, j, s], parts[1, j, s]
                     new = [ch * dh, cl * (dh + ch + dl) if i == j else ch * dl + cl * (dh + dl)]
                     acc[j] = new if s == 0 else [acc[j][0] + new[0], acc[j][1] + new[1]]
-            for j in range(i, 7):
-                pairs_of[i, j] = acc[j]
-        items = [tuple(pairs_of[q]) for q in PRODUCTS]
-        blank = (jnp.zeros((8, LANES), F32), jnp.zeros((8, LANES), F32))
-        items = items + [blank] * (32 - len(items))
-
-        def merge(a, b, mask, shift, axis):
-            size = 8 if axis == 0 else LANES
+            return {(i, j): tuple(acc[j]) for j in js}
+
+        def merge(a, b, mask, shift):
             first_in, second_in = [], []
             for u, v in zip(a, b):
-                if 2 * shift == size:
+                if shift == 4:
                     first_in.append(jnp.where(mask, u, v))
-                    second_in.append(pltpu.roll(jnp.where(mask, v, u), shift, axis))
+                    second_in.append(pltpu.roll(jnp.where(mask, v, u), shift, 0))
                 else:
-                    first_in.append(jnp.where(mask, u, pltpu.roll(v, shift, axis)))
-                    second_in.append(jnp.where(mask, pltpu.roll(u, size - shift, axis), v))
-            return add_pair(first_in, second_in)
-
-        tall = []
-        for q in range(4):
-            it = items[8 * q : 8 * q + 8]
-            one = [merge(it[r], it[r + 4], row < 4, 4, 0) for r in range(4)]
-            twice = [merge(one[r], one[r + 2], lax.rem(row, 4) < 2, 2, 0) for r in range(2)]
-            tall.append(merge(twice[0], twice[1], lax.rem(row, 2) < 1, 1, 0))
+                    first_in.append(jnp.where(mask, u, pltpu.roll(v, shift, 0)))
+                    second_in.append(jnp.where(mask, pltpu.roll(u, 8 - shift, 0), v))
+            return add_parts(tuple(first_in), tuple(second_in))
+
+        def stack(items, slots):
+            none = tuple(jnp.zeros((8, LANES), F32) for _ in next(iter(items.values())))
+            it = [items.get(q, none) for q in slots]
+            one = [merge(it[r], it[r + 4], row < 4, 4) for r in range(4)]
+            twice = [merge(one[r], one[r + 2], lax.rem(row, 4) < 2, 2) for r in range(2)]
+            return merge(twice[0], twice[1], lax.rem(row, 2) < 1, 1)
+
+        def slots_of(table, q):
+            at = {t: pair for pair, t in table.items()}
+            return [at.get(8 * q + r) for r in range(8)]
+
         quarter = lane // 32
 
-        def turned(j):
-            out = []
-            for part in range(2):
-                v = None
-                for q in range(4):
-                    u = tall[q][part]
-                    u = pltpu.roll(u, LANES - 32 * j, 1) if j else u
-                    v = u if v is None else jnp.where(quarter >= q, u, v)
-                out.append(v)
-            return out
-
-        whole = add_all([turned(j) for j in range(4)])
-        whole = add_all(
-            [[pltpu.roll(u, LANES - 8 * j, 1) if j else u for u in whole] for j in range(4)]
-        )
-        whole = add_all(
-            [
-                [pltpu.roll(u, 8 - j, 1, stride=1, stride_axis=0) for u in whole]
-                for j in range(8)
-            ]
-        )
-        keep = lax.rem(lane, 32) == row + 8
-        ends = [jnp.sum(jnp.where(keep, u, 0.0), axis=0, keepdims=True) for u in whole]
-        sums[worker] = jnp.concatenate(ends, axis=0)
+        def fold(tall):
+            def turned(j):
+                out = []
+                for part in range(len(tall[0])):
+                    v = None
+                    for q in range(len(tall)):
+                        u = tall[q][part]
+                        u = pltpu.roll(u, LANES - 32 * j, 1) if j else u
+                        v = u if v is None else jnp.where(quarter >= q, u, v)
+                    out.append(v)
+                return tuple(out)
+
+            whole = add_all([turned(j) for j in range(4)])
+            whole = add_all(
+                [
+                    tuple(pltpu.roll(u, LANES - 8 * j, 1) if j else u for u in whole)
+                    for j in range(4)
+                ]
+            )
+            whole = add_all(
+                [
+                    tuple(pltpu.roll(u, 8 - j, 1, stride=1, stride_axis=0) for u in whole)
+                    for j in range(8)
+                ]
+            )
+            keep = (lax.rem(lane, 32) == row + 8) & (quarter < len(tall))
+            return [jnp.sum(jnp.where(keep, u, 0.0), axis=0, keepdims=True) for u in whole]
+
+        items = {}
+        for k in range(STEPS):
+            divide(k)
+            for i in range(k + 1):
+                items.update(products(i, [k]))
+            if k == 3:
+                single = {q: (items[q][0] + items[q][1],) for q in EARLY}
+                early = [stack(single, slots_of(EARLY, q)) for q in range(2)]
+                first_sums[worker] = fold(early)[0]
+            if k < STEPS - 1:
+                apply(k)
+        for q in range(3):
+            high_part, low_part = stack(items, slots_of(PRODUCTS, q))
+            talls[q, 0] = high_part
+            talls[q, 1] = low_part
+        when(me != last, lambda: pl.semaphore_wait(entered, 1))
+        loop(total, lambda d: share(first_sums, 0, d))
+        apply(STEPS - 1)
+        divide(6)
+        items = {}
+        for i in range(6):
+            items.update(products(i, [6]))
+        tall = [(talls[q, 0], talls[q, 1]) for q in range(3)]
+        tall = tall + [stack(items, slots_of(PRODUCTS, 3))]
+        sums[worker] = jnp.concatenate(fold(tall), axis=0)
 
     fetched[4].wait()
     when(is_worker, work)
-    when(me != last, lambda: pl.semaphore_wait(entered, 1))
+    when(
+        jnp.logical_not(is_worker) & (me != last), lambda: pl.semaphore_wait(entered, 1)
+    )
 
     stride = plan.stride
 
-    def share(d):
-        when(
-            me != d,
-            pltpu.make_async_remote_copy(
-                src_ref=sums.at[worker],
-                dst_ref=sums.at[worker],
-                send_sem=sum_send.at[0],
-                recv_sem=sum_recv.at[0],
-                **where_is(d),
-            ).start,
-        )
-
     def give_back():
-        loop(total, share)
+        loop(total, lambda d: share(sums, 1, d))
         wide_lane = lax.broadcasted_iota(jnp.int32, (ny, LANES), 1)
         for k in range(1, 7):
             for x in range(ngx):
@@ -685,25 +729,40 @@
         accs = lax.fori_loop(0, plan.returns, collect, accs)
 
     active = plan.workers
-    when(is_worker, lambda: settle(sums.at[pl.ds(0, active - 1)], sum_recv.at[0]))
-    when(jnp.logical_not(is_worker), lambda: settle(sums, sum_recv.at[0]))
-
-    def reduce_sums():
-        zero = jnp.zeros((2, LANES), F32)
+
+    def wait_rows(ref, sem, rows):
+        while rows:
+            now = min(rows, active)
+            settle(ref.at[pl.ds(0, now)], sem)
+            rows -= now
+
+    def sent():
+        loop(n, lambda q: give(q, False))
+        wait_rows(first_sums, sum_send.at[0], total - 1)
+        wait_rows(sums, sum_send.at[1], total - 1)
+
+    loop(plan.sends, lambda j: piece(j, False))
+    when(is_worker, sent)
+
+    def landed(ref, slot):
+        when(is_worker, lambda: wait_rows(ref, sum_recv.at[slot], active - 1))
+        when(jnp.logical_not(is_worker), lambda: wait_rows(ref, sum_recv.at[slot], active))
+
+    def total_of(ref, pair):
+        zero = jnp.zeros(ref.shape[1:], F32)
+        rest = (zero,) if pair else ()
         if active <= 32:
-            return add_all([(sums[d], zero) for d in range(active)])
+            return add_all([(ref[d], *rest) for d in range(active)])
         return lax.fori_loop(
-            0, active, lambda d, a: add_pair(a, (sums[d], zero)), (zero, zero)
+            0, active, lambda d, a: add_parts(a, (ref[d], *rest)), (zero, *rest)
         )
 
-    raw_sum, lost = reduce_sums()
-    gram_high, gram_low = two_sum(raw_sum[0:1], raw_sum[1:2] + lost[0:1])
-    gram_high = jnp.broadcast_to(gram_high, (8, LANES))
-    gram_low = jnp.broadcast_to(gram_low, (8, LANES))
+    landed(first_sums, 0)
+    first_total = jnp.broadcast_to(total_of(first_sums, False)[0], (8, LANES))
 
     def entry(i, j):
-        s = place(PRODUCTS.index((min(i, j), max(i, j))))
-        return jnp.broadcast_to(gram_high[:, s : s + 1], (8, LANES))
+        s = place(EARLY[min(i, j), max(i, j)])
+        return jnp.broadcast_to(first_total[:, s : s + 1], (8, LANES))
 
     first_gram = [
         [HALF_WIDTH * entry(i, j + 1) + CHAIN[j] * entry(i, j) for j in range(3)]
@@ -720,7 +779,7 @@
         p = (ch + cl) * x
         return p, (((ch * xh - p) + ch * xl + cl * xh) + cl * xl) + rest * x
 
-    done = []
+    done, weights = [], []
     for v in range(2):
         side = [
             affine(c, lambda a, s=s: const[pl.ds((4 * s + a) * 16 + 8 * v, 8), :])
@@ -737,6 +796,14 @@
             return p, e + x * pair[1]
 
         weight = add_pair(times_pair(side[0], image[1]), times_pair(side[1], image[0]))
+        weights.append(weight)
+
+    landed(sums, 1)
+    raw_sum, lost = total_of(sums, True)
+    gram_high, gram_low = two_sum(raw_sum[0:1], raw_sum[1:2] + lost[0:1])
+    gram_high = jnp.broadcast_to(gram_high, (8, LANES))
+    gram_low = jnp.broadcast_to(gram_low, (8, LANES))
+    for weight in weights:
         high_part, low_part = two_product(gram_high, weight[0])
         pair = (high_part, low_part + (gram_high * weight[1] + gram_low * weight[0]))
         for s, times in ((32, 4), (1, 8)):
@@ -786,18 +853,6 @@
                     head = head + extra[0][0:sy] * start_part
                 out_ref[slot, cc, i] = head + (v[0:sy] + v[sy : 2 * sy])
 
-    loop(plan.sends, lambda j: piece(j, False))
-
-    def sent():
-        loop(n, lambda q: give(q, False))
-        left = total - 1
-        while left:
-            rows = min(left, active)
-            settle(sums.at[pl.ds(0, rows)], sum_send.at[0])
-            left -= rows
-
-    when(is_worker, sent)
-
 
 def per_device(displacement, load, material, free_node, table):
     shard = displacement.shape[1:]
@@ -819,7 +874,9 @@
         pltpu.VMEM((2, 7, 3 * groups * ny // 8, 8, LANES), F32),
         pltpu.VMEM((ngx, ngy, 6, sy, LANES), F32),
         pltpu.VMEM((plan.returns, 6, sy, LANES), F32),
+        pltpu.VMEM((plan.workers, 1, LANES), F32),
         pltpu.VMEM((plan.workers, 2, LANES), F32),
+        pltpu.VMEM((3, 2, 8, LANES), F32),
         pltpu.VMEM(const.shape, F32),
         pltpu.SMEM(table.shape[::-1], F32),
         pltpu.SemaphoreType.DMA((6,)),
@@ -827,8 +884,8 @@
         pltpu.SemaphoreType.DMA((2,)),
         pltpu.SemaphoreType.DMA((1,)),
         pltpu.SemaphoreType.DMA((1,)),
-        pltpu.SemaphoreType.DMA((1,)),
-        pltpu.SemaphoreType.DMA((1,)),
+        pltpu.SemaphoreType.DMA((2,)),
+        pltpu.SemaphoreType.DMA((2,)),
         pltpu.SemaphoreType.REGULAR,
     ]
     operands = (displacement, load, material, free_node, table.T, const)

time: 16.3 us -> 16.2 us (level)
  Pallas kernels: 14.9 us -> 14.7 us
where the time goes in v4:
time: 16.2 us; the launch traced here: 15.9 us
  Pallas kernels  14.7 us (91%)
  between operations  0.64 us (4%)
  local copies, waits for them, and re-layouts  0.61 us (4%)
    pallas_call x1, Pallas kernels, per_device(): pl.pallas_call(functools.partial(kernel, plan), out_shape=jax.ShapeDtypeS...  14.7 us
    squeeze x1, local copies, waits for them, and re-layouts, per_device(): return (both[0], both[1])  0.61 us

profile of v4, /device:TPU:0, one launch (start us, length us, event | category | flops | bytes accessed | tf_op | source)
XLA Modules:
  0.0 15.9 jit_solution(4320356591717004151)
XLA Ops:
  0.6 14.7 %shard_map.77 = f32[2,3,2,4,128]{4,3,2,1,0:T(4,128)S(1)} custom-call(f32[3,2,4,128]{3,2,1,0:T(4,128)} %disp_hbm.1, f32[3,2,4,128]{3,2,1,0:T(4,128)} %load_hbm.1, s32[2,4,128]{2,1,0:T(4,128)} %mat_hbm.1, s32[2,4,128]{2,1,0:T(4,128)} %free_hbm.1, f32[3,8]{1,0:T(4,128)} %bitcast.5, f32[640,128]{1,0:T(8,128)} %constant.2.clone.const_hbm), custom_call_target="tpu_custom_call" | custom-call | tf_op jit(solution)/shard_map/pallas_call | solution.py:892
  15.3 0.6 %slice_bitcast_fusion = (f32[3,2,4,128]{3,2,1,0:T(4,128)}, f32[3,2,4,128]{3,2,1,0:T(4,128)}) fusion(f32[2,3,2,4,128]{4,3,2,1,0:T(4,128)S(1)} %shard_map.77), kind=kLoop, calls=%fused_computation | loop fusion | bytes 49152 | tf_op jit(solution)/shard_map/squeeze | solution.py:902

commit v5 on v4

--- a/solution.py
+++ b/solution.py
@@ -16,13 +16,15 @@
 ORDER = (0, 3, 1, 4, 2, 5, 6, 7)
 LANES = 128
 PRODUCTS = {(i, j): t for t, (i, j) in enumerate((i, j) for i in range(6) for j in range(i, 6))}
-PRODUCTS.update({(i, 6): 24 + i for i in range(6)})
+PRODUCTS.update({(i, 6): 21 + i for i in range(5)})
+FORMS = [(i, j) for i in range(3) for j in range(3)] + [(i, None) for i in range(3)]
+SLOTS = [*PRODUCTS.items(), *(((5, 6), t) for t in range(28, 32))]
 EARLY = {(i, j): t for t, (i, j) in enumerate((i, j) for i in range(3) for j in range(i, 4))}
 F32 = jnp.float32
 
 
-def place(t):
-    return 32 * (t // 8) + 8 + t % 8
+def place(t, base):
+    return (32 * (t // 8) + base + t % 8) % LANES
 
 
 def bits(x):
@@ -32,9 +34,13 @@
     return high, top - high, (x - top.astype(np.float64)).astype(np.float32)
 
 
-def tables():
+def recurrence():
     width = 1.0 / np.float64(np.float32(1.0 / HALF_WIDTH))
-    chain = np.array([np.float64(np.float32(x / HALF_WIDTH)) * width for x in CHAIN] + [0.0])
+    return width, np.array([np.float64(np.float32(x / HALF_WIDTH)) * width for x in CHAIN] + [0.0])
+
+
+def tables(base):
+    width, chain = recurrence()
 
     def shifted(x):
         return np.concatenate([[0.0], x[:-1]])
@@ -46,12 +52,11 @@
     b = [[unit[0]] + [-times(unit[j]) for j in range(3)]]
     for j in range(2):
         b.append([(times(x) - SHIFTS[j] * x) / HALF_WIDTH for x in b[j]])
-    forms = [(i, j) for i in range(3) for j in range(3)] + [(i, None) for i in range(3)]
     wide = np.zeros((6, 4, 16, LANES))
     turn = np.zeros((3, 16, LANES))
-    for f, (i, j) in enumerate(forms):
-        for (one, two), t in PRODUCTS.items():
-            at = place(t)
+    for f, (i, j) in enumerate(FORMS):
+        for (one, two), t in SLOTS:
+            at = place(t, base)
             turn[:, f, at] = (1.0, 1.0, 0.0) if j is None else (chain[one], chain[two], width)
             for a in range(4):
                 left, right = b[i][a], b[j or 0][a]
@@ -212,6 +217,7 @@
     first_sums,
     sums,
     talls,
+    square,
     const,
     table_ref,
     in_sem,
@@ -500,7 +506,7 @@
 
         rows8 = [pl.ds(8 * r, 8) for r in range(ny // 8)]
 
-        def apply(j):
+        def stress(j):
             grad = gradient([[basis[j, c, g] * fields[0, g] for g in span] for c in range(3)])
             pio = [[[[None] * len(rows8) for _ in span] for _ in range(3)] for _ in range(3)]
             for g in span:
@@ -521,8 +527,12 @@
                         for b in range(3):
                             v = sum(f[i][k] * t[k, b] for k in range(3))
                             pio[i][b][g][r] = v + sum(d[i][k] * s[k, b] for k in range(3))
+            pio = [[[jnp.concatenate(pio[c][b][g], axis=0) for g in span] for b in range(3)] for c in range(3)]
+            return grad, pio
+
+        def scatter(j, pio):
             for c in range(3):
-                e = [[jnp.concatenate(pio[c][b][g], axis=0) for g in span] for b in range(3)]
+                e = pio[c]
                 wide = add(e[0], last_y(e[0]))
                 tilt = sub(last_y(e[1]), e[1])
                 rise = add(e[2], last_y(e[2]))
@@ -536,6 +546,9 @@
                         fields[2, g] - CHAIN[j] / HALF_WIDTH
                     ) * basis[j, c, g]
 
+        def apply(j):
+            scatter(j, stress(j)[1])
+
         mine = (depth >= halo) & (depth < halo + own) & (plane < plan.nz)
         spots = [(c, g, r) for c in range(3) for g in span for r in range(ny // 8)]
         mine = [mine[8 * r : 8 * r + 8] for r in range(ny // 8)]
@@ -600,17 +613,12 @@
             whole = add_all([turned(j) for j in range(4)])
             whole = add_all(
                 [
-                    tuple(pltpu.roll(u, LANES - 8 * j, 1) if j else u for u in whole)
-                    for j in range(4)
+                    tuple(pltpu.roll(u, own - j, 1, stride=1, stride_axis=0) for u in whole)
+                    for j in range(own)
                 ]
             )
-            whole = add_all(
-                [
-                    tuple(pltpu.roll(u, 8 - j, 1, stride=1, stride_axis=0) for u in whole)
-                    for j in range(8)
-                ]
-            )
-            keep = (lax.rem(lane, 32) == row + 8) & (quarter < len(tall))
+            keep = lax.rem(lane + (2 * LANES - halo - own) - row, 32) == 0
+            keep = keep & (lax.rem(lane + (LANES - halo - own) - row, LANES) < 32 * len(tall))
             return [jnp.sum(jnp.where(keep, u, 0.0), axis=0, keepdims=True) for u in whole]
 
         items = {}
@@ -624,20 +632,39 @@
                 first_sums[worker] = fold(early)[0]
             if k < STEPS - 1:
                 apply(k)
-        for q in range(3):
+        width, chain = recurrence()
+        for i in range(5):
+            up, same = items[i + 1, 5], items[i, 5]
+            factor = float((chain[i] - chain[5]) / width)
+            high_part, low_part = two_sum(up[0], factor * same[0])
+            items[i, 6] = (high_part, low_part + (up[1] + factor * same[1]))
+        for q in range(4):
             high_part, low_part = stack(items, slots_of(PRODUCTS, q))
             talls[q, 0] = high_part
             talls[q, 1] = low_part
+        square[0] = items[5, 5][0]
+        square[1] = items[5, 5][1]
         when(me != last, lambda: pl.semaphore_wait(entered, 1))
         loop(total, lambda d: share(first_sums, 0, d))
-        apply(STEPS - 1)
-        divide(6)
-        items = {}
-        for i in range(6):
-            items.update(products(i, [6]))
+        grad, pio = stress(5)
+        energy = None
+        for g in span:
+            dense = sum(pio[c][b][g] * grad[c][b][g] for c in range(3) for b in range(3))
+            for r in range(ny // 8):
+                v = [basis[5, c, g, rows8[r]] for c in range(3)]
+                nodes = fields[2, g, rows8[r]] * (v[0] * v[0] + v[1] * v[1] + v[2] * v[2])
+                u = dense[8 * r : 8 * r + 8] * (1.0 / HALF_WIDTH) + nodes
+                u = jnp.where(mine[r], u, 0.0)
+                energy = u if energy is None else energy + u
+        factor = float(-chain[5] / width)
+        high_part, low_part = two_sum(energy, factor * square[0])
+        ends = (high_part, low_part + factor * square[1])
+        ends = add_pair(ends, [pltpu.roll(u, 4, 0) for u in ends])
         tall = [(talls[q, 0], talls[q, 1]) for q in range(3)]
-        tall = tall + [stack(items, slots_of(PRODUCTS, 3))]
+        tall.append(tuple(jnp.where(row < 4, talls[3, p], ends[p]) for p in range(2)))
         sums[worker] = jnp.concatenate(fold(tall), axis=0)
+        loop(total, lambda d: share(sums, 1, d))
+        scatter(5, pio)
 
     fetched[4].wait()
     when(is_worker, work)
@@ -648,7 +675,6 @@
     stride = plan.stride
 
     def give_back():
-        loop(total, lambda d: share(sums, 1, d))
         wide_lane = lax.broadcasted_iota(jnp.int32, (ny, LANES), 1)
         for k in range(1, 7):
             for x in range(ngx):
@@ -761,7 +787,7 @@
     first_total = jnp.broadcast_to(total_of(first_sums, False)[0], (8, LANES))
 
     def entry(i, j):
-        s = place(EARLY[min(i, j), max(i, j)])
+        s = place(EARLY[min(i, j), max(i, j)], halo + own)
         return jnp.broadcast_to(first_total[:, s : s + 1], (8, LANES))
 
     first_gram = [
@@ -779,7 +805,11 @@
         p = (ch + cl) * x
         return p, (((ch * xh - p) + ch * xl + cl * xh) + cl * xl) + rest * x
 
-    done, weights = [], []
+    def times_pair(x, pair):
+        p, e = two_product(x, pair[0])
+        return p, e + x * pair[1]
+
+    weights = []
     for v in range(2):
         side = [
             affine(c, lambda a, s=s: const[pl.ds((4 * s + a) * 16 + 8 * v, 8), :])
@@ -790,19 +820,14 @@
             add_pair(scaled(turn[q], 8, side[2 + q]), scaled(turn[2], 8, side[4 + q]))
             for q in range(2)
         ]
-
-        def times_pair(x, pair):
-            p, e = two_product(x, pair[0])
-            return p, e + x * pair[1]
-
-        weight = add_pair(times_pair(side[0], image[1]), times_pair(side[1], image[0]))
-        weights.append(weight)
+        weights.append(add_pair(times_pair(side[0], image[1]), times_pair(side[1], image[0])))
 
     landed(sums, 1)
     raw_sum, lost = total_of(sums, True)
     gram_high, gram_low = two_sum(raw_sum[0:1], raw_sum[1:2] + lost[0:1])
     gram_high = jnp.broadcast_to(gram_high, (8, LANES))
     gram_low = jnp.broadcast_to(gram_low, (8, LANES))
+    done = []
     for weight in weights:
         high_part, low_part = two_product(gram_high, weight[0])
         pair = (high_part, low_part + (gram_high * weight[1] + gram_low * weight[0]))
@@ -810,13 +835,15 @@
             pair = add_all(
                 [[pltpu.roll(u, LANES - s * q, 1) if q else u for u in pair] for q in range(times)]
             )
-        done.append(jnp.broadcast_to((pair[0] + pair[1])[:, 8:9], (8, LANES)))
-
-    def form(f):
-        return jnp.broadcast_to(done[f // 8][f % 8 : f % 8 + 1], (8, LANES))
-
-    gram = [[form(3 * i + j) for j in range(3)] for i in range(3)]
-    d = solve_small(gram, [form(9 + i) for i in range(3)])
+        done.append(
+            jnp.broadcast_to((pair[0] + pair[1])[:, halo + own : halo + own + 1], (8, LANES))
+        )
+    form = {
+        q: jnp.broadcast_to(done[f // 8][f % 8 : f % 8 + 1], (8, LANES))
+        for f, q in enumerate(FORMS)
+    }
+    gram = [[form[i, j] for j in range(3)] for i in range(3)]
+    d = solve_small(gram, [form[i, None] for i in range(3)])
     base_at = 24 * 16 + 9 * 16
     vector = affine(c, lambda a: const[pl.ds(base_at + 8 * a, 8), :])
     moved = affine(c, lambda a: const[pl.ds(base_at + 32 + 8 * a, 8), :])
@@ -826,31 +853,21 @@
     coef = times_pair(factor, image)
     coef = add_pair(coef, [pltpu.roll(u, 6, 0) for u in coef])
     coef = add_pair(coef, [pltpu.roll(u, 7, 0) for u in coef])
-    coef = two_sum(coef[0][0:1], coef[1][0:1])
-
-    def spread_coef(part, k):
-        return jnp.broadcast_to(coef[part][:, k : k + 1], (8, LANES))
+    coef = coef[0][0:1] + coef[1][0:1]
+
+    def spread_coef(k):
+        return jnp.broadcast_to(coef[:, k : k + 1], (8, LANES))
 
     for slot in range(2):
-        sets = [[-spread_coef(0, 32 + k) for k in range(7)]]
-        if slot == 1:
-            sets = [[spread_coef(part, k) for k in range(7)] for part in range(2)]
-        duo = [
-            [jnp.where(row < sy, w[k + 1], w[k + 2]) for w in sets] for k in range(0, 6, 2)
-        ]
+        w = [spread_coef(k) if slot else -spread_coef(32 + k) for k in range(7)]
+        duo = [jnp.where(row < sy, w[k + 1], w[k + 2]) for k in range(0, 6, 2)]
         for cc in range(3):
             for i in range(sx):
                 v = None
                 for k in range(0, 6, 2):
-                    held_k = accs[mates.index((k, cc, i))]
-                    u = duo[k // 2][0] * held_k
-                    for extra in duo[k // 2][1:]:
-                        u = u + extra * held_k
+                    u = duo[k // 2] * accs[mates.index((k, cc, i))]
                     v = u if v is None else v + u
-                start_part = raw[3 + cc, i] * raw[7, i]
-                head = sets[0][0][0:sy] * start_part
-                for extra in sets[1:]:
-                    head = head + extra[0][0:sy] * start_part
+                head = w[0][0:sy] * (raw[3 + cc, i] * raw[7, i])
                 out_ref[slot, cc, i] = head + (v[0:sy] + v[sy : 2 * sy])
 
 
@@ -862,7 +879,7 @@
     ngx, ngy, ngz = grid
     ny = ngy * sy
     groups = plan.groups
-    const = jnp.asarray(tables())
+    const = jnp.asarray(tables(plan.halo + plan.own))
     buffers = [
         pltpu.VMEM((FIELDS, sx, sy, sz), F32),
         pltpu.VMEM((2, sx, sy, sz), jnp.int32),
@@ -876,7 +893,8 @@
         pltpu.VMEM((plan.returns, 6, sy, LANES), F32),
         pltpu.VMEM((plan.workers, 1, LANES), F32),
         pltpu.VMEM((plan.workers, 2, LANES), F32),
-        pltpu.VMEM((3, 2, 8, LANES), F32),
+        pltpu.VMEM((4, 2, 8, LANES), F32),
+        pltpu.VMEM((2, 8, LANES), F32),
         pltpu.VMEM(const.shape, F32),
         pltpu.SMEM(table.shape[::-1], F32),
         pltpu.SemaphoreType.DMA((6,)),

time: 16.2 us -> 16 us (0.988)
  Pallas kernels: 14.7 us -> 14.5 us
    pallas_call x1, Pallas kernels: 14.7 us -> 14.5 us  [per_device(): pl.pallas_call(functools.partial(kernel, plan), out_shape=jax.ShapeDtypeS...]
where the time goes in v5:
time: 16 us; the launch traced here: 15.8 us
  Pallas kernels  14.5 us (91%)
  between operations  0.64 us (4%)
  local copies, waits for them, and re-layouts  0.61 us (4%)
    pallas_call x1, Pallas kernels, per_device(): pl.pallas_call(functools.partial(kernel, plan), out_shape=jax.ShapeDtypeS...  14.5 us
    squeeze x1, local copies, waits for them, and re-layouts, per_device(): return (both[0], both[1])  0.61 us

profile of v5, /device:TPU:0, one launch (start us, length us, event | category | flops | bytes accessed | tf_op | source)
XLA Modules:
  0.0 15.8 jit_solution(17332569737140398062)
XLA Ops:
  0.6 14.5 %shard_map.77 = f32[2,3,2,4,128]{4,3,2,1,0:T(4,128)S(1)} custom-call(f32[3,2,4,128]{3,2,1,0:T(4,128)} %disp_hbm.1, f32[3,2,4,128]{3,2,1,0:T(4,128)} %load_hbm.1, s32[2,4,128]{2,1,0:T(4,128)} %mat_hbm.1, s32[2,4,128]{2,1,0:T(4,128)} %free_hbm.1, f32[3,8]{1,0:T(4,128)} %bitcast.5, f32[640,128]{1,0:T(8,128)} %constant.2.clone.const_hbm), custom_call_target="tpu_custom_call" | custom-call | tf_op jit(solution)/shard_map/pallas_call | solution.py:910
  15.2 0.6 %slice_bitcast_fusion = (f32[3,2,4,128]{3,2,1,0:T(4,128)}, f32[3,2,4,128]{3,2,1,0:T(4,128)}) fusion(f32[2,3,2,4,128]{4,3,2,1,0:T(4,128)S(1)} %shard_map.77), kind=kLoop, calls=%fused_computation | loop fusion | bytes 49152 | tf_op jit(solution)/shard_map/squeeze | solution.py:920

commit v6 on v5

--- a/solution.py
+++ b/solution.py
@@ -183,7 +183,7 @@
         self.from_high = [(sz * z + sz - 1) // own for z in range(ngz)]
         self.sends = max(b - a + 1 for a, b in zip(self.to_low, self.to_high))
         self.returns = max(b - a + 1 for a, b in zip(self.from_low, self.from_high))
-        assert sz == LANES and 8 == 2 * sy and own <= self.stride and LANES % self.pitch == 0
+        assert sz == LANES and 8 == 2 * sy and own <= self.stride and halo + own <= 56
 
 
 def pick(values, z):
@@ -347,7 +347,7 @@
 
     def piece(j, start):
         valid, slot, d = routes[j] if routes else route(j)
-        dst = recv.at[slot, :, gx, gy]
+        dst = recv.at[slot, gx, gy]
         remote = pltpu.make_async_remote_copy(
             src_ref=pack.at[j],
             dst_ref=dst,
@@ -397,7 +397,7 @@
         seg = sx * pitch
 
         def gather_rows(slot, k, x):
-            return jnp.concatenate([recv[slot, k, x, g] for g in range(ngy)], axis=0)
+            return jnp.concatenate([recv[slot, x, g, k] for g in range(ngy)], axis=0)
 
         def source(k, x):
             return jnp.where(near, gather_rows(0, k, x), gather_rows(1, k, x))
@@ -827,17 +827,20 @@
     gram_high, gram_low = two_sum(raw_sum[0:1], raw_sum[1:2] + lost[0:1])
     gram_high = jnp.broadcast_to(gram_high, (8, LANES))
     gram_low = jnp.broadcast_to(gram_low, (8, LANES))
-    done = []
+    halves = []
     for weight in weights:
         high_part, low_part = two_product(gram_high, weight[0])
         pair = (high_part, low_part + (gram_high * weight[1] + gram_low * weight[0]))
-        for s, times in ((32, 4), (1, 8)):
-            pair = add_all(
-                [[pltpu.roll(u, LANES - s * q, 1) if q else u for u in pair] for q in range(times)]
-            )
-        done.append(
-            jnp.broadcast_to((pair[0] + pair[1])[:, halo + own : halo + own + 1], (8, LANES))
+        halves.append(
+            add_all([[pltpu.roll(u, LANES - 32 * q, 1) if q else u for u in pair] for q in range(4)])
         )
+    pair = [jnp.where(lane < 64, u, v) for u, v in zip(*halves)]
+    pair = add_all([[pltpu.roll(u, LANES - q, 1) if q else u for u in pair] for q in range(8)])
+    value = pair[0] + pair[1]
+    done = []
+    for v in range(2):
+        at = halo + own + 64 * v
+        done.append(jnp.broadcast_to(value[:, at : at + 1], (8, LANES)))
     form = {
         q: jnp.broadcast_to(done[f // 8][f % 8 : f % 8 + 1], (8, LANES))
         for f, q in enumerate(FORMS)
@@ -868,7 +871,7 @@
                     u = duo[k // 2] * accs[mates.index((k, cc, i))]
                     v = u if v is None else v + u
                 head = w[0][0:sy] * (raw[3 + cc, i] * raw[7, i])
-                out_ref[slot, cc, i] = head + (v[0:sy] + v[sy : 2 * sy])
+                out_ref[slot, cc, sy * i : sy * (i + 1)] = head + (v[0:sy] + v[sy : 2 * sy])
 
 
 def per_device(displacement, load, material, free_node, table):
@@ -884,7 +887,7 @@
         pltpu.VMEM((FIELDS, sx, sy, sz), F32),
         pltpu.VMEM((2, sx, sy, sz), jnp.int32),
         pltpu.VMEM((plan.sends, plan.tiles, sy, LANES), F32),
-        pltpu.VMEM((2, plan.tiles, ngx, ngy, sy, LANES), F32),
+        pltpu.VMEM((2, ngx, ngy, plan.tiles, sy, LANES), F32),
         pltpu.VMEM((7, 3, groups, ny, LANES), F32),
         pltpu.VMEM((3, groups, ny, LANES), F32),
         pltpu.VMEM((17, groups, ny, LANES), F32),
@@ -909,7 +912,7 @@
     operands = (displacement, load, material, free_node, table.T, const)
     both = pl.pallas_call(
         functools.partial(kernel, plan),
-        out_shape=jax.ShapeDtypeStruct((2,) + displacement.shape, F32),
+        out_shape=jax.ShapeDtypeStruct((2, 3, sx * sy, sz), F32),
         in_specs=[pl.BlockSpec(memory_space=pltpu.HBM)] * 6,
         out_specs=pl.BlockSpec(memory_space=pltpu.VMEM),
         scratch_shapes=buffers,
@@ -917,7 +920,7 @@
             collective_id=0, has_side_effects=True, vmem_limit_bytes=32 << 20
         ),
     )(*(pltpu.with_memory_space_constraint(a, pltpu.HBM) for a in operands))
-    return both[0], both[1]
+    return both[0].reshape(displacement.shape), both[1].reshape(displacement.shape)
 
 
 def solution(mesh):

time: 16 us -> 16 us (level)
    slice x0 -> x1, local copies, waits for them, and re-layouts: none -> 0.61 us  [per_device(): both[1].reshape(displacement.shape)]
    squeeze x1 -> x0, local copies, waits for them, and re-layouts: 0.61 us -> none  [per_device(): return (both[0], both[1])]
where the time goes in v6:
time: 16 us; the launch traced here: 15.8 us
  Pallas kernels  14.5 us (91%)
  between operations  0.64 us (4%)
  local copies, waits for them, and re-layouts  0.61 us (4%)
    pallas_call x1, Pallas kernels, per_device(): pl.pallas_call(functools.partial(kernel, plan), out_shape=jax.ShapeDtypeS...  14.5 us
    slice x1, local copies, waits for them, and re-layouts, per_device(): both[1].reshape(displacement.shape)  0.61 us

profile of v6, /device:TPU:0, one launch (start us, length us, event | category | flops | bytes accessed | tf_op | source)
XLA Modules:
  0.0 15.8 jit_solution(6795145032537684120)
XLA Ops:
  0.6 14.5 %shard_map.77 = f32[2,3,8,128]{3,2,1,0:T(8,128)S(1)} custom-call(f32[3,2,4,128]{3,2,1,0:T(4,128)} %disp_hbm.1, f32[3,2,4,128]{3,2,1,0:T(4,128)} %load_hbm.1, s32[2,4,128]{2,1,0:T(4,128)} %mat_hbm.1, s32[2,4,128]{2,1,0:T(4,128)} %free_hbm.1, f32[3,8]{1,0:T(4,128)} %bitcast.5, f32[640,128]{1,0:T(8,128)} %constant.2.clone.const_hbm), custom_call_target="tpu_custom_call" | custom-call | tf_op jit(solution)/shard_map/pallas_call | solution.py:913
  15.2 0.6 %fusion = (f32[1,3,8,128]{3,2,1,0:T(8,128)}, f32[1,3,8,128]{3,2,1,0:T(8,128)}) fusion(f32[2,3,8,128]{3,2,1,0:T(8,128)S(1)} %shard_map.77), kind=kLoop, calls=%fused_computation | loop fusion | bytes 49152 | tf_op jit(solution)/shard_map/slice | solution.py:923

commit v7 on v6

--- a/solution.py
+++ b/solution.py
@@ -18,7 +18,6 @@
 PRODUCTS = {(i, j): t for t, (i, j) in enumerate((i, j) for i in range(6) for j in range(i, 6))}
 PRODUCTS.update({(i, 6): 21 + i for i in range(5)})
 FORMS = [(i, j) for i in range(3) for j in range(3)] + [(i, None) for i in range(3)]
-SLOTS = [*PRODUCTS.items(), *(((5, 6), t) for t in range(28, 32))]
 EARLY = {(i, j): t for t, (i, j) in enumerate((i, j) for i in range(3) for j in range(i, 4))}
 F32 = jnp.float32
 
@@ -39,7 +38,7 @@
     return width, np.array([np.float64(np.float32(x / HALF_WIDTH)) * width for x in CHAIN] + [0.0])
 
 
-def tables(base):
+def tables(plan):
     width, chain = recurrence()
 
     def shifted(x):
@@ -52,11 +51,14 @@
     b = [[unit[0]] + [-times(unit[j]) for j in range(3)]]
     for j in range(2):
         b.append([(times(x) - SHIFTS[j] * x) / HALF_WIDTH for x in b[j]])
+    base = plan.halo + plan.own
+    lanes = [(*q, place(t, base)) for q, t in PRODUCTS.items()]
+    lanes += [(5, 6, at) for at in range(LANES) if plan.halo <= at % plan.pitch < base]
+    assert len({at for _, _, at in lanes}) == len(lanes)
     wide = np.zeros((6, 4, 16, LANES))
     turn = np.zeros((3, 16, LANES))
     for f, (i, j) in enumerate(FORMS):
-        for (one, two), t in SLOTS:
-            at = place(t, base)
+        for one, two, at in lanes:
             turn[:, f, at] = (1.0, 1.0, 0.0) if j is None else (chain[one], chain[two], width)
             for a in range(4):
                 left, right = b[i][a], b[j or 0][a]
@@ -632,20 +634,19 @@
                 first_sums[worker] = fold(early)[0]
             if k < STEPS - 1:
                 apply(k)
+            if k == 3:
+                when(me != last, lambda: pl.semaphore_wait(entered, 1))
+                loop(total, lambda d: share(first_sums, 0, d))
         width, chain = recurrence()
         for i in range(5):
             up, same = items[i + 1, 5], items[i, 5]
             factor = float((chain[i] - chain[5]) / width)
             high_part, low_part = two_sum(up[0], factor * same[0])
             items[i, 6] = (high_part, low_part + (up[1] + factor * same[1]))
-        for q in range(4):
-            high_part, low_part = stack(items, slots_of(PRODUCTS, q))
-            talls[q, 0] = high_part
-            talls[q, 1] = low_part
+        tall = [stack(items, slots_of(PRODUCTS, q)) for q in range(4)]
+        talls[...] = jnp.concatenate(fold(tall), axis=0)
         square[0] = items[5, 5][0]
         square[1] = items[5, 5][1]
-        when(me != last, lambda: pl.semaphore_wait(entered, 1))
-        loop(total, lambda d: share(first_sums, 0, d))
         grad, pio = stress(5)
         energy = None
         for g in span:
@@ -659,10 +660,9 @@
         factor = float(-chain[5] / width)
         high_part, low_part = two_sum(energy, factor * square[0])
         ends = (high_part, low_part + factor * square[1])
-        ends = add_pair(ends, [pltpu.roll(u, 4, 0) for u in ends])
-        tall = [(talls[q, 0], talls[q, 1]) for q in range(3)]
-        tall.append(tuple(jnp.where(row < 4, talls[3, p], ends[p]) for p in range(2)))
-        sums[worker] = jnp.concatenate(fold(tall), axis=0)
+        for shift in (4, 2, 1):
+            ends = add_pair(ends, [pltpu.roll(u, shift, 0) for u in ends])
+        sums[worker] = talls[...] + jnp.concatenate([u[0:1] for u in ends], axis=0)
         loop(total, lambda d: share(sums, 1, d))
         scatter(5, pio)
 
@@ -835,12 +835,12 @@
             add_all([[pltpu.roll(u, LANES - 32 * q, 1) if q else u for u in pair] for q in range(4)])
         )
     pair = [jnp.where(lane < 64, u, v) for u, v in zip(*halves)]
-    pair = add_all([[pltpu.roll(u, LANES - q, 1) if q else u for u in pair] for q in range(8)])
+    for s, times in ((8, 4), (1, 8)):
+        pair = add_all(
+            [[pltpu.roll(u, LANES - s * q, 1) if q else u for u in pair] for q in range(times)]
+        )
     value = pair[0] + pair[1]
-    done = []
-    for v in range(2):
-        at = halo + own + 64 * v
-        done.append(jnp.broadcast_to(value[:, at : at + 1], (8, LANES)))
+    done = [jnp.broadcast_to(value[:, 64 * v : 64 * v + 1], (8, LANES)) for v in range(2)]
     form = {
         q: jnp.broadcast_to(done[f // 8][f % 8 : f % 8 + 1], (8, LANES))
         for f, q in enumerate(FORMS)
@@ -882,7 +882,7 @@
     ngx, ngy, ngz = grid
     ny = ngy * sy
     groups = plan.groups
-    const = jnp.asarray(tables(plan.halo + plan.own))
+    const = jnp.asarray(tables(plan))
     buffers = [
         pltpu.VMEM((FIELDS, sx, sy, sz), F32),
         pltpu.VMEM((2, sx, sy, sz), jnp.int32),
@@ -896,7 +896,7 @@
         pltpu.VMEM((plan.returns, 6, sy, LANES), F32),
         pltpu.VMEM((plan.workers, 1, LANES), F32),
         pltpu.VMEM((plan.workers, 2, LANES), F32),
-        pltpu.VMEM((4, 2, 8, LANES), F32),
+        pltpu.VMEM((2, LANES), F32),
         pltpu.VMEM((2, 8, LANES), F32),
         pltpu.VMEM(const.shape, F32),
         pltpu.SMEM(table.shape[::-1], F32),

time: 16 us -> 15.9 us (level)
  no operation moved by 1% of the time
where the time goes in v7:
time: 15.9 us; the launch traced here: 15.7 us
  Pallas kernels  14.5 us (91%)
  between operations  0.64 us (4%)
  local copies, waits for them, and re-layouts  0.61 us (4%)
    pallas_call x1, Pallas kernels, per_device(): pl.pallas_call(functools.partial(kernel, plan), out_shape=jax.ShapeDtypeS...  14.5 us
    slice x1, local copies, waits for them, and re-layouts, per_device(): both[1].reshape(displacement.shape)  0.61 us

profile of v7, /device:TPU:0, one launch (start us, length us, event | category | flops | bytes accessed | tf_op | source)
XLA Modules:
  0.0 15.7 jit_solution(15718695285670121359)
XLA Ops:
  0.6 14.5 %shard_map.77 = f32[2,3,8,128]{3,2,1,0:T(8,128)S(1)} custom-call(f32[3,2,4,128]{3,2,1,0:T(4,128)} %disp_hbm.1, f32[3,2,4,128]{3,2,1,0:T(4,128)} %load_hbm.1, s32[2,4,128]{2,1,0:T(4,128)} %mat_hbm.1, s32[2,4,128]{2,1,0:T(4,128)} %free_hbm.1, f32[3,8]{1,0:T(4,128)} %bitcast.5, f32[640,128]{1,0:T(8,128)} %constant.2.clone.const_hbm), custom_call_target="tpu_custom_call" | custom-call | tf_op jit(solution)/shard_map/pallas_call | solution.py:913
  15.1 0.6 %fusion = (f32[1,3,8,128]{3,2,1,0:T(8,128)}, f32[1,3,8,128]{3,2,1,0:T(8,128)}) fusion(f32[2,3,8,128]{3,2,1,0:T(8,128)S(1)} %shard_map.77), kind=kLoop, calls=%fused_computation | loop fusion | bytes 49152 | tf_op jit(solution)/shard_map/slice | solution.py:923

commit v8 on v6

--- a/solution.py
+++ b/solution.py
@@ -598,7 +598,7 @@
 
         quarter = lane // 32
 
-        def fold(tall):
+        def squeeze(tall):
             def turned(j):
                 out = []
                 for part in range(len(tall[0])):
@@ -610,7 +610,9 @@
                     out.append(v)
                 return tuple(out)
 
-            whole = add_all([turned(j) for j in range(4)])
+            return add_all([turned(j) for j in range(4)])
+
+        def spread(whole, count):
             whole = add_all(
                 [
                     tuple(pltpu.roll(u, own - j, 1, stride=1, stride_axis=0) for u in whole)
@@ -618,7 +620,7 @@
                 ]
             )
             keep = lax.rem(lane + (2 * LANES - halo - own) - row, 32) == 0
-            keep = keep & (lax.rem(lane + (LANES - halo - own) - row, LANES) < 32 * len(tall))
+            keep = keep & (lax.rem(lane + (LANES - halo - own) - row, LANES) < 32 * count)
             return [jnp.sum(jnp.where(keep, u, 0.0), axis=0, keepdims=True) for u in whole]
 
         items = {}
@@ -629,7 +631,7 @@
             if k == 3:
                 single = {q: (items[q][0] + items[q][1],) for q in EARLY}
                 early = [stack(single, slots_of(EARLY, q)) for q in range(2)]
-                first_sums[worker] = fold(early)[0]
+                first_sums[worker] = spread(squeeze(early), 2)[0]
             if k < STEPS - 1:
                 apply(k)
         width, chain = recurrence()
@@ -638,10 +640,11 @@
             factor = float((chain[i] - chain[5]) / width)
             high_part, low_part = two_sum(up[0], factor * same[0])
             items[i, 6] = (high_part, low_part + (up[1] + factor * same[1]))
-        for q in range(4):
-            high_part, low_part = stack(items, slots_of(PRODUCTS, q))
-            talls[q, 0] = high_part
-            talls[q, 1] = low_part
+        ready = squeeze([stack(items, slots_of(PRODUCTS, q)) for q in range(3)])
+        fourth = stack(items, slots_of(PRODUCTS, 3))
+        for part in range(2):
+            talls[0, part] = ready[part]
+            talls[1, part] = fourth[part]
         square[0] = items[5, 5][0]
         square[1] = items[5, 5][1]
         when(me != last, lambda: pl.semaphore_wait(entered, 1))
@@ -660,9 +663,9 @@
         high_part, low_part = two_sum(energy, factor * square[0])
         ends = (high_part, low_part + factor * square[1])
         ends = add_pair(ends, [pltpu.roll(u, 4, 0) for u in ends])
-        tall = [(talls[q, 0], talls[q, 1]) for q in range(3)]
-        tall.append(tuple(jnp.where(row < 4, talls[3, p], ends[p]) for p in range(2)))
-        sums[worker] = jnp.concatenate(fold(tall), axis=0)
+        newest = squeeze([tuple(jnp.where(row < 4, talls[1, p], ends[p]) for p in range(2))])
+        whole = tuple(jnp.where(quarter == 3, newest[p], talls[0, p]) for p in range(2))
+        sums[worker] = jnp.concatenate(spread(whole, 4), axis=0)
         loop(total, lambda d: share(sums, 1, d))
         scatter(5, pio)
 
@@ -896,7 +899,7 @@
         pltpu.VMEM((plan.returns, 6, sy, LANES), F32),
         pltpu.VMEM((plan.workers, 1, LANES), F32),
         pltpu.VMEM((plan.workers, 2, LANES), F32),
-        pltpu.VMEM((4, 2, 8, LANES), F32),
+        pltpu.VMEM((2, 2, 8, LANES), F32),
         pltpu.VMEM((2, 8, LANES), F32),
         pltpu.VMEM(const.shape, F32),
         pltpu.SMEM(table.shape[::-1], F32),

time: 16 us -> 16.1 us (level)
  no operation moved by 1% of the time
where the time goes in v8:
time: 16.1 us; the launch traced here: 15.8 us
  Pallas kernels  14.6 us (91%)
  between operations  0.64 us (4%)
  local copies, waits for them, and re-layouts  0.61 us (4%)
    pallas_call x1, Pallas kernels, per_device(): pl.pallas_call(functools.partial(kernel, plan), out_shape=jax.ShapeDtypeS...  14.6 us
    slice x1, local copies, waits for them, and re-layouts, per_device(): both[1].reshape(displacement.shape)  0.61 us

profile of v8, /device:TPU:0, one launch (start us, length us, event | category | flops | bytes accessed | tf_op | source)
XLA Modules:
  0.0 15.8 jit_solution(563114643420173323)
XLA Ops:
  0.6 14.6 %shard_map.77 = f32[2,3,8,128]{3,2,1,0:T(8,128)S(1)} custom-call(f32[3,2,4,128]{3,2,1,0:T(4,128)} %disp_hbm.1, f32[3,2,4,128]{3,2,1,0:T(4,128)} %load_hbm.1, s32[2,4,128]{2,1,0:T(4,128)} %mat_hbm.1, s32[2,4,128]{2,1,0:T(4,128)} %free_hbm.1, f32[3,8]{1,0:T(4,128)} %bitcast.5, f32[640,128]{1,0:T(8,128)} %constant.2.clone.const_hbm), custom_call_target="tpu_custom_call" | custom-call | tf_op jit(solution)/shard_map/pallas_call | solution.py:916
  15.2 0.6 %fusion = (f32[1,3,8,128]{3,2,1,0:T(8,128)}, f32[1,3,8,128]{3,2,1,0:T(8,128)}) fusion(f32[2,3,8,128]{3,2,1,0:T(8,128)S(1)} %shard_map.77), kind=kLoop, calls=%fused_computation | loop fusion | bytes 49152 | tf_op jit(solution)/shard_map/slice | solution.py:926
